TPU v7x, 256 devices: a whole 4x4x8 slice. The times are simulated.
256 devices in a mesh: gx: 128 (over x, z, y), bl: 2 (over core).
Axes of the slice: x: 4, y: 4, z: 8, core: 2. Of those that a mesh axis runs over, the one named last changes fastest.
Arguments:
- voltages: bfloat16 [2, 1024, 71680], P('bl', 'gx'), may hold values from -10 to 10, as said below
- model_magnitude: float32 [128, 2048], P('gx'), may hold values from 0.06 to 0.25
- model_phase: float32 [128, 2048], P('gx'), may hold values from -3.140625 to 3.140625
Outputs:
- visibilities: bfloat16 [128, 2, 2048, 2048], P('gx', None, 'bl')
- gains: float32 [2, 2, 1024, 128], P(None, 'bl', 'gx')
Inputs may be any that keep to these rules, and one draw needn't show every extreme that they name: `voltages`: each input's sampled voltage stream.
All inputs are finite; a program needn't handle non-finite values.
Results may differ from a plain program's by a relative error of at most 0.0057.
Values may be sent and summed in bfloat16 or wider, within the bound.
No kernel may reach another device: no remote copies, remote signals or barrier semaphores. Data moves between devices by JAX's collectives and lax.ppermute only.
A program may use at most 64 MiB of HBM per device.

v0:
```python
import math

import jax
import jax.numpy as jnp
from jax import lax
from jax.sharding import PartitionSpec as P

NFFT = 2048
TAPS = 4
ITERS = 4


epsilon = 1e-06


def window_table(tap_count, length):
    positions = jnp.arange(tap_count * length, dtype=jnp.float32)
    centre = (positions + 0.5) / length - tap_count / 2.0
    hann_taper = 0.5 - 0.5 * jnp.cos(2.0 * math.pi * (positions + 0.5) / (tap_count * length))
    return (jnp.sinc(centre) * hann_taper).reshape(tap_count, length)


def channel_table(channels, stride, length):
    bin_index = jnp.arange(channels, dtype=jnp.int32) * stride + (stride + 1) // 2
    sample_index = jnp.arange(length, dtype=jnp.int32)
    phase_index = bin_index[:, None] * sample_index[None, :] % length
    angles = phase_index.astype(jnp.float32) * (2.0 * math.pi / length)
    factor = 1.0 / math.sqrt(length)
    return jnp.stack([jnp.cos(angles) * factor, -jnp.sin(angles) * factor], axis=1)


def stack_left(row_block):
    real_part = row_block[:, 0]
    imag_part = row_block[:, 1]
    upper = jnp.concatenate([real_part, imag_part], axis=2)
    lower = jnp.concatenate([imag_part, -real_part], axis=2)
    return jnp.stack([upper, lower], axis=1)


def on_device(voltages, model_magnitude, model_phase):
    groups = lax.axis_size("gx")
    local_channels = model_magnitude.shape[0]
    channels = local_channels * groups
    inputs = model_magnitude.shape[1]
    half_rows = inputs // lax.axis_size("bl")
    owned_inputs = voltages.shape[1]
    frames_total = voltages.shape[2] // NFFT
    spectra = frames_total - TAPS + 1
    taps_window = window_table(TAPS, NFFT)
    blocks = voltages.reshape(owned_inputs, frames_total, NFFT)
    frames = blocks[:, 0:spectra, :].astype(jnp.float32) * taps_window[0]
    for tap_index in range(1, TAPS):
        frames = (
            frames
            + blocks[:, tap_index : tap_index + spectra, :].astype(jnp.float32)
            * taps_window[tap_index]
        )
    stride = NFFT // 2 // channels
    transform = channel_table(channels, stride, NFFT).reshape(2 * channels, NFFT)
    spectra_local = lax.dot_general(
        transform,
        frames.reshape(owned_inputs * spectra, NFFT),
        (((1,), (1,)), ((), ())),
        precision=lax.Precision.HIGHEST,
        preferred_element_type=jnp.float32,
    )
    spectra_local = spectra_local.reshape(channels, 2, owned_inputs, spectra).astype(jnp.bfloat16)
    tile_index = lax.axis_index("bl")
    row_start = tile_index * half_rows
    own_rows = lax.all_to_all(spectra_local, "gx", split_axis=0, concat_axis=2, tiled=True)
    left_side = stack_left(own_rows)
    portion = lax.all_gather(own_rows, "bl", axis=2, tiled=True)
    right_side = jnp.concatenate([portion[:, 0], portion[:, 1]], axis=2)
    block_power = jnp.einsum(
        "cohk,crk->cohr", left_side, right_side, preferred_element_type=jnp.float32
    )
    whole_inputs = portion
    cross_sum, whole_inputs = (block_power, whole_inputs)
    cross_power = cross_sum * (1.0 / spectra)
    model_real = model_magnitude * jnp.cos(model_phase)
    model_imag = model_magnitude * jnp.sin(model_phase)
    inverse_square = 1.0 / (model_magnitude * model_magnitude)
    highest = lax.Precision.HIGHEST
    dense_values = whole_inputs.astype(jnp.float32)
    diagonal = jnp.sum(dense_values * dense_values, axis=(1, 3)) * (1.0 / spectra)

    def apply_power(probe_real, probe_imag):
        inner_real = jnp.einsum(
            "cps,cp->cs", dense_values[:, 0], probe_real, precision=highest
        ) + jnp.einsum("cps,cp->cs", dense_values[:, 1], probe_imag, precision=highest)
        inner_imag = jnp.einsum(
            "cps,cp->cs", dense_values[:, 0], probe_imag, precision=highest
        ) - jnp.einsum("cps,cp->cs", dense_values[:, 1], probe_real, precision=highest)
        real_out = (
            jnp.einsum("cps,cs->cp", dense_values[:, 0], inner_real, precision=highest)
            - jnp.einsum("cps,cs->cp", dense_values[:, 1], inner_imag, precision=highest)
        ) * (1.0 / spectra) - diagonal * probe_real
        imag_out = (
            jnp.einsum("cps,cs->cp", dense_values[:, 0], inner_imag, precision=highest)
            + jnp.einsum("cps,cs->cp", dense_values[:, 1], inner_real, precision=highest)
        ) * (1.0 / spectra) - diagonal * probe_imag
        return (real_out, imag_out)

    def single_step(gain_real, gain_imag):
        probe_real = gain_real * model_real - gain_imag * model_imag
        probe_imag = gain_real * model_imag + gain_imag * model_real
        image_real, image_imag = apply_power(probe_real, probe_imag)
        energy = (
            jnp.sum(probe_real * probe_real + probe_imag * probe_imag, axis=1, keepdims=True)
            + epsilon
        )
        factor = inverse_square / energy
        fresh_real = (image_real * model_real + image_imag * model_imag) * factor
        fresh_imag = (image_imag * model_real - image_real * model_imag) * factor
        return (fresh_real, fresh_imag)

    def double_step(pair_index, current):
        first_real, first_imag = single_step(current[0], current[1])
        fresh_real, fresh_imag = single_step(first_real, first_imag)
        return ((fresh_real + first_real) * 0.5, (fresh_imag + first_imag) * 0.5)

    start_gains = (
        jnp.ones((local_channels, inputs), jnp.float32),
        jnp.zeros((local_channels, inputs), jnp.float32),
    )
    gain_real, gain_imag = lax.fori_loop(0, ITERS // 2, double_step, start_gains)
    gain_pair = jnp.stack([gain_real, gain_imag], axis=1)
    own_gains = lax.dynamic_slice_in_dim(gain_pair, row_start, half_rows, 2)
    owned_gains = lax.all_to_all(own_gains, "gx", split_axis=2, concat_axis=0, tiled=True)
    gain_output = jnp.transpose(owned_gains, (1, 2, 0))[:, None]
    return (cross_power.astype(jnp.bfloat16), gain_output)


def solution(mesh):
    in_specs = (P("bl", "gx", None), P("gx", None), P("gx", None))
    out_specs = (P("gx", None, "bl", None), P(None, "bl", "gx", None))
    return jax.shard_map(
        on_device, mesh=mesh, in_specs=in_specs, out_specs=out_specs, check_vma=False
    )
```

profile of v0, /device:TPU:1, one launch (start us, length us, event | category | flops | bytes accessed | tf_op | source)
XLA Modules:
  0.0 104.1 jit_solution(16863530753998408993)
XLA Ops:
  0.6 0.0 copy-start
  0.6 0.2 fusion.97
  0.8 4.2 %cosine_multiply_fusion = (f32[128,1,2048]{2,0,1:T(8,128)S(1)}, f32[128,1,2048]{2,0,1:T(8,128)S(1)}) fusion(s32[128]{0:T(128)S(1)} %multiply_add_fusion.3), kind=kLoop, calls=%fused_computation.120 | loop fusion | flops 4456448 | bytes 2097664 | tf_op jit(solution)/shard_map/mul | solution.py:29
  5.0 0.0 copy-done
  5.0 0.5 fusion.110
  5.6 0.0 copy-start.1
  5.6 0.0 copy-start.2
  5.6 7.8 %fusion.72 = bf16[128,2,8,32]{0,3,2,1:T(8,128)(2,1)S(1)} fusion(f32[128,1,2048]{2,0,1:T(8,128)S(1)} %get-tuple-element.156, f32[128,1,2048]{2,0,1:T(8,128)S(1)} %get-tuple-element.155, bf16[8,32,2048]{2,0,1:T(8,128)(2,1)S(1)} %get-tuple-element.141, bf16[8,32,2048]{2,0,1:T(8,128)(2,1)S(1)} %get-tuple-element.139, ...), kind=kOutput, calls=%fused_computation.107 | convolution fusion | flops 1616969728 | bytes 6455296 | tf_op jit(solution)/shard_map/dot_general | solution.py:60
  13.4 0.4 copy.36
  13.9 1.0 reshape.336
  14.9 16.3 %all-to-all-start = ((bf16[128,2,256]{2,1,0:T(2,128)(2,1)}), bf16[128,2,256]{2,1,0:T(2,128)(2,1)S(1)}, u32[]{:S(2)}, u32[]{:S(2)}) async-start(bf16[128,2,256]{2,1,0:T(2,128)(2,1)} %reshape.336), calls=%async_computation | async-start | bytes 262144 | tf_op jit(solution)/shard_map/all_to_all | solution.py:70
  31.3 0.2 sine_multiply_fusion
  31.5 10.6 %all-to-all-done = bf16[128,2,256]{2,1,0:T(2,128)(2,1)S(1)} async-done(((bf16[128,2,256]{2,1,0:T(2,128)(2,1)}), bf16[128,2,256]{2,1,0:T(2,128)(2,1)S(1)}, u32[]{:S(2)}, u32[]{:S(2)}) %all-to-all-start) | async-done | bytes 131104 | tf_op jit(solution)/shard_map/all_to_all | solution.py:70
  42.2 0.3 reshape.337
  42.5 0.2 copy.38
  42.7 3.8 %all_gather.3 = bf16[1,2,2048,32]{2,3,1,0:T(8,128)(2,1)S(1)} all-gather(bf16[1,2,1024,32]{2,3,1,0:T(8,128)(2,1)S(1)} %copy.38), channel_id=1, replica_groups=mesh['gx'=128,'bl'=2] {'bl'}, dimensions={2}, use_global_device_ids=true | all-gather | bytes 393216 | tf_op jit(solution)/shard_map/all_gather | solution.py:72
  46.5 0.1 multiply_reduce_fusion
  46.6 0.3 copy.41
  47.0 30.6 %while.13 = (s32[]{:T(128)}, f32[1,2048]{1,0:T(1,128)S(1)}, f32[1,2048]{1,0:T(1,128)S(1)}, f32[1,2048]{1,0:T(1,128)S(1)}, f32[1,2048]{1,0:T(1,128)S(1)}, /*index...) while((s32[]{:T(128)}, f32[1,2048]{1,0:T(1,128)S(1)}, ...), condition=%wide.region_4.5_spmd.clone, body=%wide.region_1.4_spmd.clone.sunk | while | flops 12705923 | bytes 17259680 | solution.py:126
  47.0 0.6 add_reduce_fusion.4
  48.3 0.6 convolution_bitcast_fusion.12
  48.9 0.6 fusion.197
  49.5 0.6 convolution_bitcast_fusion.13
  50.1 0.6 fusion.199
  50.8 0.9 fusion.201
  51.7 0.9 fusion.200
  52.6 0.9 fusion.202
  53.6 0.9 fusion.198
  54.6 0.7 add_reduce_fusion.5
  55.9 0.6 convolution_bitcast_fusion.14
  56.5 0.6 fusion.203
  57.1 0.6 convolution_bitcast_fusion.15
  57.7 0.6 fusion.205
  58.4 0.9 fusion.207
  59.3 0.9 fusion.206
  60.3 0.9 fusion.208
  61.2 0.9 fusion.204
  62.2 0.1 add_multiply_fusion.11
  62.3 0.6 add_reduce_fusion.4
  63.6 0.6 convolution_bitcast_fusion.12
  64.2 0.6 fusion.197
  64.8 0.6 convolution_bitcast_fusion.13
  65.4 0.6 fusion.199
  66.0 0.9 fusion.201
  67.0 0.9 fusion.200
  67.9 0.9 fusion.202
  68.9 0.9 fusion.198
  69.8 0.7 add_reduce_fusion.5
  71.2 0.6 convolution_bitcast_fusion.14
  71.8 0.6 fusion.203
  72.4 0.6 convolution_bitcast_fusion.15
  73.0 0.6 fusion.205
  73.7 0.9 fusion.207
  74.6 0.9 fusion.206
  75.6 0.9 fusion.208
  76.5 0.9 fusion.204
  77.5 0.1 add_multiply_fusion.11
  77.5 0.1 fusion.106
  77.6 1.0 copy.42
  78.7 6.4 %all-to-all-start.1 = ((f32[1,2,1024]{1,0,2:T(1,128)}), f32[1,2,1024]{1,0,2:T(1,128)S(1)}, u32[]{:S(2)}, u32[]{:S(2)}) async-start(f32[1,2,1024]{1,0,2:T(1,128)} %copy.42), calls=%async_computation.1 | async-start | bytes 1048576 | tf_op jit(solution)/shard_map/all_to_all | solution.py:129
  85.1 5.8 %fusion.56 = bf16[1,2,1024,2048]{3,2,1,0:T(8,128)(2,1)} fusion(bf16[1,1,1024,64]{2,3,1,0:T(8,128)(2,1)S(1)} %get-tuple-element.147, bf16[1,1,1024,64]{2,3,1,0:T(8,128)(2,1)S(1)} %get-tuple-element.146, bf16[1,2048,32]{1,2,0:T(8,128)(2,1)S(1)} %get-tuple-element.143, bf16[1,2048,32]{1,2,0:T(8,128)(2,1)S(1)} %get-tuple-element.142), kind=kOutput, calls=%fused_computation.87 | convolution fusion | flops 545914880 | bytes 8912896 | tf_op jit(solution)/shard_map/cohk,crk->cohr/dot_general | solution.py:74
  90.9 11.7 %all-to-all-done.1 = f32[1,2,1024]{1,0,2:T(1,128)S(1)} async-done(((f32[1,2,1024]{1,0,2:T(1,128)}), f32[1,2,1024]{1,0,2:T(1,128)S(1)}, u32[]{:S(2)}, u32[]{:S(2)}) %all-to-all-start.1) | async-done | bytes 8224 | tf_op jit(solution)/shard_map/all_to_all | solution.py:129
  102.6 0.9 copy.46
  103.4 0.7 copy.44
  (20 shorter events, 0.2 us)
Async XLA Ops:
  0.6 4.4 %copy-start = (bf16[1,8,71680]{2,1,0:T(8,128)(2,1)S(1)}, bf16[1,8,71680]{2,1,0:T(8,128)(2,1)}, u32[]{:S(2)}) copy-start(bf16[1,8,71680]{2,1,0:T(8,128)(2,1)} %param.5) | copy-start | bytes 3440644
  5.6 25.7 %copy-start.1 = (f32[1,2048]{1,0:T(1,128)S(1)}, f32[1,2048]{1,0:T(1,128)}, u32[]{:S(2)}) copy-start(f32[1,2048]{1,0:T(1,128)} %param.6) | copy-start | bytes 24580
  5.6 25.7 %copy-start.2 = (f32[1,2048]{1,0:T(1,128)S(1)}, f32[1,2048]{1,0:T(1,128)}, u32[]{:S(2)}) copy-start(f32[1,2048]{1,0:T(1,128)} %param.7) | copy-start | bytes 24580
  14.9 27.3 %all-to-all-start = ((bf16[128,2,256]{2,1,0:T(2,128)(2,1)}), bf16[128,2,256]{2,1,0:T(2,128)(2,1)S(1)}, u32[]{:S(2)}, u32[]{:S(2)}) async-start(bf16[128,2,256]{2,1,0:T(2,128)(2,1)} %reshape.336), calls=%async_computation | async-start | bytes 262144 | tf_op jit(solution)/shard_map/all_to_all | solution.py:70
  78.7 23.9 %all-to-all-start.1 = ((f32[1,2,1024]{1,0,2:T(1,128)}), f32[1,2,1024]{1,0,2:T(1,128)S(1)}, u32[]{:S(2)}, u32[]{:S(2)}) async-start(f32[1,2,1024]{1,0,2:T(1,128)} %copy.42), calls=%async_computation.1 | async-start | bytes 1048576 | tf_op jit(solution)/shard_map/all_to_all | solution.py:129
where the time goes:
time: 104 us
  matrix products  38.7 us (37%)
  starting transfers between devices  22.7 us (22%)
  waiting for transfers between devices  22.4 us (22%)
  other arithmetic  7.61 us (7%)
  local copies, waits for them, and re-layouts  5.46 us (5%)
  blocking collectives  3.79 us (4%)
  loops' own time  2.68 us (3%)
    all_to_all x1, starting transfers between devices, on_device(): lax.all_to_all(spectra_local, 'gx', split_axis=0, concat_axis=2, tiled=True)  16.3 us
    all_to_all x1, waiting for transfers between devices, on_device(): lax.all_to_all(own_gains, 'gx', split_axis=2, concat_axis=0, tiled=True)  11.7 us
    all_to_all x1, waiting for transfers between devices, on_device(): lax.all_to_all(spectra_local, 'gx', split_axis=0, concat_axis=2, tiled=True)  10.6 us
    dot_general x1, matrix products, on_device(): lax.dot_general(transform, frames.reshape(owned_inputs * spectra, NFFT),...  7.82 us
    all_to_all x1, starting transfers between devices, on_device(): lax.all_to_all(own_gains, 'gx', split_axis=2, concat_axis=0, tiled=True)  6.38 us
    dot_general x1, matrix products, on_device(): jnp.einsum('cohk,crk->cohr', left_side, right_side, preferred_element_typ...  5.77 us
    mul x1, other arithmetic, channel_table(): jnp.cos(angles) * factor  4.2 us
    dot_general x4, matrix products, apply_power(): jnp.einsum('cps,cs->cp', dense_values[:, 1], inner_imag, precision=highest)  3.8 us
  transfers between devices with their start and end apart: 2, of which 2 were waited for; matrix products, arithmetic and copies ran while one was open for 6% of the time, Pallas kernels for 0%

commit v1 on v0

v1 whole, which is shorter than its diff:
```python
import functools
import math

import jax
import jax.numpy as jnp
import numpy as np
from jax import lax
from jax.experimental import pallas as pl
from jax.experimental.pallas import tpu as pltpu
from jax.sharding import PartitionSpec as P

NFFT = 2048
TAPS = 4
SPECTRA = 32
ITERS = 4
CHANNELS = 128
OWNED = 8
EPSILON = 1e-06
F32 = jnp.float32
BF16 = jnp.bfloat16
FOLD = 256
FOLDS = NFFT // FOLD


def split_bf16(values):
    high = values.astype(np.float32).astype(jnp.bfloat16)
    low = (values - high.astype(np.float64)).astype(np.float32).astype(jnp.bfloat16)
    return high, low


def fold_weights():
    position = np.arange(TAPS * NFFT, dtype=np.float64) + 0.5
    hann = 0.5 - 0.5 * np.cos(2.0 * np.pi * position / (TAPS * NFFT))
    taper = np.sinc(position / NFFT - TAPS / 2.0) * hann
    taper = taper.reshape(TAPS, FOLDS, FOLD)
    signs = (-1.0) ** np.arange(FOLDS)
    folded = (taper * signs[None, :, None]).transpose(1, 0, 2)
    return folded.astype(np.float32)


def transform_weights():
    odd = 2 * np.arange(CHANNELS) + 1
    phase = (odd[:, None] * np.arange(FOLD)[None, :]) % (2 * FOLD)
    angle = phase.astype(np.float64) * (2.0 * np.pi / (2 * FOLD))
    scale = 1.0 / math.sqrt(NFFT)
    table = np.concatenate([np.cos(angle), -np.sin(angle)], axis=0) * scale
    high, low = split_bf16(table)
    return np.concatenate([high, high, low], axis=1)


def channelize_kernel(volts_ref, window_ref, table_ref, out_ref, folded_ref, rows_ref):
    for part in range(FOLD // 128):

        def fold_step(fold, sums):
            start = pl.multiple_of(fold * FOLD + part * 128, 128)
            taps = [
                jnp.broadcast_to(
                    window_ref[fold, tap : tap + 1, part * 128 : part * 128 + 128],
                    (OWNED, 128),
                )
                for tap in range(TAPS)
            ]
            sums = list(sums)
            for frame in range(SPECTRA + TAPS - 1):
                piece = volts_ref[:, pl.ds(start + frame * NFFT, 128)].astype(F32)
                for tap in range(TAPS):
                    s = frame - tap
                    if 0 <= s < SPECTRA:
                        sums[s] = sums[s] + piece * taps[tap]
            return tuple(sums)

        zero = jnp.zeros((OWNED, 128), F32)
        sums = lax.fori_loop(0, FOLDS, fold_step, (zero,) * SPECTRA)
        for s in range(SPECTRA):
            folded_ref[part, pl.ds(s * OWNED, OWNED), :] = sums[s]
    pieces = []
    for part in range(FOLD // 128):
        pieces.append(
            jnp.concatenate(
                [folded_ref[part, pl.ds(j, SPECTRA, OWNED), :] for j in range(OWNED)],
                axis=0,
            )
        )
    folded = jnp.concatenate(pieces, axis=1)
    high = folded.astype(BF16)
    low = (folded - high.astype(F32)).astype(BF16)
    right = jnp.concatenate([high, low, high], axis=1)
    spectra = lax.dot_general(
        table_ref[...], right, (((1,), (1,)), ((), ())), preferred_element_type=F32
    )
    for part in range(2):
        for side in range(2):
            rows_ref[pl.ds(part * 2 + side, CHANNELS, 4), :] = spectra[
                part * CHANNELS : (part + 1) * CHANNELS, side * 128 : side * 128 + 128
            ]
    out_ref[...] = rows_ref[...].astype(BF16)


def channelize(volts):
    return pl.pallas_call(
        channelize_kernel,
        out_shape=jax.ShapeDtypeStruct((CHANNELS * 4, 128), BF16),
        scratch_shapes=[
            pltpu.VMEM((2, SPECTRA * OWNED, 128), F32),
            pltpu.VMEM((CHANNELS * 4, 128), F32),
        ],
        compiler_params=pltpu.CompilerParams(vmem_limit_bytes=16 * 2**20),
        name="channelize",
    )(volts, jnp.asarray(fold_weights()), jnp.asarray(transform_weights()))


def solve_kernel(
    own_ref, other_ref, mreal_ref, mimag_ref, inverse_ref, out_ref,
    wide_ref, xr_ref, xi_ref, probe_ref, part_ref,
):
    half = lax.axis_index("bl")
    for side, source in ((0, own_ref), (1, other_ref)):
        tile = half if side == 0 else 1 - half
        wide_ref[...] = source[...].astype(F32)
        for part in range(2):
            target = xr_ref if part == 0 else xi_ref
            for group in range(2):
                block = wide_ref[pl.ds(part * 2 + group, 128, 4), :].T
                for j in range(4):
                    target[tile * OWNED + group * 4 + j] = block[j * 32 : j * 32 + 32, :]
    tiles = 2 * OWNED

    def gathered(which):
        total = part_ref[which, pl.ds(0, tiles, 8), :]
        for row in range(1, 8):
            total = total + part_ref[which, pl.ds(row, tiles, 8), :]
        return total

    def eight(values):
        return (values[0:8] + values[8:16]) + (values[16:24] + values[24:32])

    for tile in range(tiles):
        real, imag = xr_ref[tile], xi_ref[tile]
        part_ref[0, tile * 8 : tile * 8 + 8, :] = eight(real * real + imag * imag)
    diagonal = gathered(0) * (1.0 / SPECTRA)
    mreal, mimag, inverse = mreal_ref[...], mimag_ref[...], inverse_ref[...]

    def single_step(greal, gimag):
        yreal = greal * mreal - gimag * mimag
        yimag = greal * mimag + gimag * mreal
        energy = jnp.sum(yreal * yreal + yimag * yimag, keepdims=True) + EPSILON
        factor = inverse / energy
        probe_ref[0] = yreal
        probe_ref[1] = yimag
        areal = jnp.zeros((SPECTRA, 128), F32)
        aimag = jnp.zeros((SPECTRA, 128), F32)
        for tile in range(tiles):
            real, imag = xr_ref[tile], xi_ref[tile]
            pr = jnp.broadcast_to(probe_ref[0, tile : tile + 1, :], (SPECTRA, 128))
            pi = jnp.broadcast_to(probe_ref[1, tile : tile + 1, :], (SPECTRA, 128))
            areal = areal + (real * pr + imag * pi)
            aimag = aimag + (real * pi - imag * pr)
        sreal = jnp.broadcast_to(jnp.sum(areal, axis=1, keepdims=True), (SPECTRA, 128))
        simag = jnp.broadcast_to(jnp.sum(aimag, axis=1, keepdims=True), (SPECTRA, 128))
        for tile in range(tiles):
            real, imag = xr_ref[tile], xi_ref[tile]
            rows = slice(tile * 8, tile * 8 + 8)
            part_ref[0, rows, :] = eight(real * sreal - imag * simag)
            part_ref[1, rows, :] = eight(real * simag + imag * sreal)
        wreal = gathered(0) * (1.0 / SPECTRA) - diagonal * yreal
        wimag = gathered(1) * (1.0 / SPECTRA) - diagonal * yimag
        return (
            (wreal * mreal + wimag * mimag) * factor,
            (wimag * mreal - wreal * mimag) * factor,
        )

    greal = jnp.ones((tiles, 128), F32)
    gimag = jnp.zeros((tiles, 128), F32)

    def double_step(_, gains):
        first = single_step(*gains)
        fresh = single_step(*first)
        return tuple((a + b) * 0.5 for a, b in zip(fresh, first))

    greal, gimag = lax.fori_loop(0, ITERS // 2, double_step, (greal, gimag))
    probe_ref[0] = greal
    probe_ref[1] = gimag
    start = pl.multiple_of(half * OWNED, OWNED)
    wide_ref[0:128, :] = jnp.zeros((128, 128), F32)
    wide_ref[0:8, :] = probe_ref[0, pl.ds(start, OWNED), :]
    wide_ref[8:16, :] = probe_ref[1, pl.ds(start, OWNED), :]
    out_ref[...] = wide_ref[0:128, :].T


def solve(own, other, mreal, mimag, inverse):
    tiles = 2 * OWNED
    return pl.pallas_call(
        solve_kernel,
        out_shape=jax.ShapeDtypeStruct((128, 128), F32),
        scratch_shapes=[
            pltpu.VMEM((512, 128), F32),
            pltpu.VMEM((tiles, SPECTRA, 128), F32),
            pltpu.VMEM((tiles, SPECTRA, 128), F32),
            pltpu.VMEM((2, tiles, 128), F32),
            pltpu.VMEM((2, tiles * 8, 128), F32),
        ],
        compiler_params=pltpu.CompilerParams(vmem_limit_bytes=16 * 2**20),
        name="solve",
    )(own, other, mreal, mimag, inverse)


ROWS = 128


def power_kernel(own_ref, other_ref, out_ref, wide_ref, line_ref, upper_ref, lower_ref, right_ref):
    half = lax.axis_index("bl")
    step = pl.program_id(0)

    @pl.when(step == 0)
    def _():
        for side, source in ((0, own_ref), (1, other_ref)):
            tile = half if side == 0 else 1 - half
            wide_ref[...] = source[...].astype(F32)
            for group in range(2):
                real = wide_ref[pl.ds(group, 128, 4), :]
                imag = wide_ref[pl.ds(2 + group, 128, 4), :]
                for j in range(4):
                    a = real[:, j * 32 : j * 32 + 32]
                    b = imag[:, j * 32 : j * 32 + 32]
                    line_ref[pl.ds(group * 4 + j, 128, OWNED), :] = jnp.concatenate(
                        [a, b, b, -a], axis=1
                    )
            lines = line_ref[...]
            start = pl.multiple_of(tile * 1024, 1024)
            right_ref[pl.ds(start, 1024), :] = lines[:, 0:64].astype(BF16)
            if side == 0:
                scaled = lines * (1.0 / SPECTRA)
                upper_ref[...] = scaled[:, 0:64].astype(BF16)
                lower_ref[...] = scaled[:, 64:128].astype(BF16)

    rows = pl.ds(pl.multiple_of(step * ROWS, ROWS), ROWS)
    for part, left in ((0, upper_ref), (1, lower_ref)):
        out_ref[part] = lax.dot_general(
            left[rows, :], right_ref[...], (((1,), (1,)), ((), ())),
            preferred_element_type=F32,
        ).astype(BF16)


def power(own, other):
    return pl.pallas_call(
        power_kernel,
        grid=(1024 // ROWS,),
        in_specs=[pl.BlockSpec((512, 128), lambda s: (0, 0))] * 2,
        out_specs=pl.BlockSpec((2, ROWS, 2048), lambda s: (0, s, 0)),
        out_shape=jax.ShapeDtypeStruct((2, 1024, 2048), BF16),
        scratch_shapes=[
            pltpu.VMEM((512, 128), F32),
            pltpu.VMEM((1024, 128), F32),
            pltpu.VMEM((1024, 64), BF16),
            pltpu.VMEM((1024, 64), BF16),
            pltpu.VMEM((2048, 64), BF16),
        ],
        compiler_params=pltpu.CompilerParams(vmem_limit_bytes=24 * 2**20),
        cost_estimate=pl.CostEstimate(
            flops=2 * 2 * 1024 * 2048 * 64, bytes_accessed=9 * 2**20, transcendentals=0
        ),
        name="power",
    )(own, other)


def turn_kernel(gains_ref, out_ref):
    turned = gains_ref[...].T
    out_ref[0, 0] = turned[0:8, :]
    out_ref[1, 0] = turned[8:16, :]


def on_device(voltages, model_magnitude, model_phase):
    spectra = channelize(voltages[0])
    own = lax.all_to_all(spectra.reshape(CHANNELS, 4, 128), "gx", 0, 0)
    own = own.reshape(512, 128)
    other = lax.ppermute(own, "bl", [(0, 1), (1, 0)])

    def tiles(values):
        return values.reshape(2, 128, OWNED).transpose(0, 2, 1).reshape(2 * OWNED, 128)

    mreal = tiles(model_magnitude * jnp.cos(model_phase))
    mimag = tiles(model_magnitude * jnp.sin(model_phase))
    inverse = tiles(1.0 / (model_magnitude * model_magnitude))
    gains = solve(own, other, mreal, mimag, inverse)
    moved = lax.all_to_all(gains.reshape(128, 1, 128), "gx", 0, 0)
    visible = power(own, other)
    gain_output = pl.pallas_call(
        turn_kernel,
        out_shape=jax.ShapeDtypeStruct((2, 1, OWNED, CHANNELS), F32),
        name="turn",
    )(moved.reshape(128, 128))
    return visible[None], gain_output


def solution(mesh):
    in_specs = (P("bl", "gx", None), P("gx", None), P("gx", None))
    out_specs = (P("gx", None, "bl", None), P(None, "bl", "gx", None))
    return jax.shard_map(
        on_device, mesh=mesh, in_specs=in_specs, out_specs=out_specs, check_vma=False
    )
```

time: 104 us -> 56.9 us (0.55)
  matrix products: 38.7 us -> 0 us
  blocking collectives: 3.79 us -> 27.1 us
  waiting for transfers between devices: 22.4 us -> 3.66 us
  starting transfers between devices: 22.7 us -> 8.29 us
  Pallas kernels: 0 us -> 11.6 us
  other arithmetic: 7.61 us -> 1.01 us
  loops' own time: 2.68 us -> 0 us
  local copies, waits for them, and re-layouts: 5.46 us -> 4.11 us
    dot_general x34 -> x0, matrix products: 38.7 us -> none  [the longest x1 7.82 us: on_device(): lax.dot_general(transform, frames.reshape(owned_inputs * spectra, NFFT),...]
    all_to_all x0 -> x1, blocking collectives: none -> 27.1 us  [on_device(): own = lax.all_to_all(spectra.reshape(CHANNELS, 4, 128), 'gx', 0, 0)]
    all_to_all x2 -> x1, waiting for transfers between devices: 22.4 us -> 3.66 us  [on_device(): moved = lax.all_to_all(gains.reshape(128, 1, 128), 'gx', 0, 0)]
    all_to_all x2 -> x1, starting transfers between devices: 22.7 us -> 6.17 us  [on_device(): moved = lax.all_to_all(gains.reshape(128, 1, 128), 'gx', 0, 0)]
    pallas_call x0 -> x4, Pallas kernels: none -> 11.6 us  [the longest x1 6.92 us: power(): pl.pallas_call(power_kernel, grid=(1024 // ROWS,), in_specs=[pl.BlockSpec...]
    mul x14 -> x1, other arithmetic: 4.8 us -> 1.01 us  [on_device(): mimag = tiles(model_magnitude * jnp.sin(model_phase))]
    all_gather x1 -> x0, blocking collectives: 3.79 us -> none  [on_device(): portion = lax.all_gather(own_rows, 'bl', axis=2, tiled=True)]
    reduce_sum x5 -> x0, other arithmetic: 2.69 us -> none  [the longest x4 2.62 us: single_step(): jnp.sum(probe_real * probe_real + probe_imag * probe_imag, axis=1, keepdi...]
  transfers between devices with their start and end apart: 2 -> 2, of which waited for: 2 -> 1; matrix products, arithmetic and copies ran while one was open for 6% -> 3% of each run, Pallas kernels for 0% -> 12%
where the time goes in v1:
time: 56.9 us; the launch traced here: 56.5 us
  blocking collectives  27.1 us (48%)
  Pallas kernels  11.6 us (20%)
  starting transfers between devices  8.29 us (15%)
  local copies, waits for them, and re-layouts  4.11 us (7%)
  waiting for transfers between devices  3.66 us (6%)
  other arithmetic  1.01 us (2%)
  between operations  0.69 us (1%)
    all_to_all x1, blocking collectives, on_device(): own = lax.all_to_all(spectra.reshape(CHANNELS, 4, 128), 'gx', 0, 0)  27.1 us
    pallas_call x1, Pallas kernels, power(): pl.pallas_call(power_kernel, grid=(1024 // ROWS,), in_specs=[pl.BlockSpec...  6.92 us
    all_to_all x1, starting transfers between devices, on_device(): moved = lax.all_to_all(gains.reshape(128, 1, 128), 'gx', 0, 0)  6.17 us
    all_to_all x1, waiting for transfers between devices, on_device(): moved = lax.all_to_all(gains.reshape(128, 1, 128), 'gx', 0, 0)  3.66 us
    unnamed x8, local copies, waits for them, and re-layouts  3.62 us
    ppermute x1, starting transfers between devices, on_device(): other = lax.ppermute(own, 'bl', [(0, 1), (1, 0)])  2.12 us
    pallas_call x1, Pallas kernels, solve(): pl.pallas_call(solve_kernel, out_shape=jax.ShapeDtypeStruct((128, 128), F...  2 us
    pallas_call x1, Pallas kernels, on_device(): pl.pallas_call(turn_kernel, out_shape=jax.ShapeDtypeStruct((2, 1, OWNED,...  1.51 us
  transfers between devices with their start and end apart: 2, of which 1 were waited for; matrix products, arithmetic and copies ran while one was open for 3% of the time, Pallas kernels for 12%

profile of v1, /device:TPU:1, one launch (start us, length us, event | category | flops | bytes accessed | tf_op | source)
XLA Modules:
  0.0 56.5 jit_solution(14325364218682781121)
XLA Ops:
  0.6 0.0 copy-start
  0.6 1.2 %copy-done = bf16[1,8,71680]{2,1,0:T(8,128)(2,1)S(1)} copy-done((bf16[1,8,71680]{2,1,0:T(8,128)(2,1)S(1)}, bf16[1,8,71680]{2,1,0:T(8,128)(2,1)}, u32[]{:S(2)}) %copy-start) | copy-done | bytes 1146904
  1.9 0.0 copy-start.1
  1.9 1.0 %copy-done.1 = bf16[256,768]{1,0:T(8,128)(2,1)S(1)} copy-done((bf16[256,768]{1,0:T(8,128)(2,1)S(1)}, bf16[256,768]{1,0:T(8,128)(2,1)}, u32[]{:S(2)}) %copy-start.1) | copy-done | bytes 393240
  2.9 0.0 copy-start.2
  2.9 0.8 %copy-done.2 = f32[8,4,256]{2,1,0:T(4,128)S(1)} copy-done((f32[8,4,256]{2,1,0:T(4,128)S(1)}, f32[8,4,256]{2,1,0:T(4,128)}, u32[]{:S(2)}) %copy-start.2) | copy-done | bytes 32792
  3.6 1.1 %channelize.1 = bf16[512,128]{1,0:T(8,128)(2,1)S(1)} custom-call(bf16[8,71680]{1,0:T(8,128)(2,1)S(1)} %bitcast.17, f32[8,4,256]{2,1,0:T(4,128)S(1)} %copy-done.2, bf16[256,768]{1,0:T(8,128)(2,1)S(1)} %copy-done.1), custom_call_target="tpu_custom_call" | custom-call | tf_op jit(solution)/shard_map/channelize/pallas_call | solution.py:100
  4.8 27.1 %all_to_all.10 = bf16[128,4,128]{2,1,0:T(4,128)(2,1)S(1)} all-to-all(bf16[128,4,128]{2,1,0:T(4,128)(2,1)S(1)} %bitcast.18), channel_id=1, replica_groups=mesh['gx'=128,'bl'=2] {'gx'}, dimensions={0} | all-to-all | bytes 262144 | tf_op jit(solution)/shard_map/all_to_all | solution.py:274
  31.9 2.1 %collective-permute-start = (bf16[512,128]{1,0:T(8,128)(2,1)S(1)}, bf16[512,128]{1,0:T(8,128)(2,1)S(1)}, u32[]{:S(2)}, u32[]{:S(2)}) collective-permute-start(bf16[512,128]{1,0:T(8,128)(2,1)S(1)} %bitcast.14), channel_id=1, source_target_pairs={{0,1},{1,0},{2,3},{3,2},{4,5},{5,4},{6,7},{7,6},{8,9},{9,8},{10,11... | collective-permute-start | bytes 393224 | tf_op jit(solution)/shard_map/ppermute | solution.py:276
  34.0 1.0 %multiply_reduce_fusion = (f32[2048]{0:T(1024)S(1)}, f32[2048]{0:T(1024)S(1)}, f32[2048]{0:T(1024)S(1)}) fusion(f32[1,2048]{1,0:T(1,128)} %param.6, f32[1,2048]{1,0:T(1,128)} %param.7), kind=kLoop, calls=%fused_computation.1 | loop fusion | flops 8192 | bytes 40960 | tf_op jit(solution)/shard_map/mul | solution.py:282
  35.1 0.1 reshape.38
  35.2 0.1 copy.14
  35.2 0.1 reshape.36
  35.3 0.1 copy.13
  35.4 0.1 reshape.40
  35.5 0.1 copy.15
  35.6 0.0 collective-permute-done.other_ref
  35.6 2.0 %solve.1 = f32[128,128]{1,0:T(8,128)} custom-call(bf16[512,128]{1,0:T(8,128)(2,1)S(1)} %bitcast.15, bf16[512,128]{1,0:T(8,128)(2,1)S(1)} %collective-permute-done.other_ref, f32[16,128]{1,0:T(8,128)S(1)} %bitcast.20, f32[16,128]{1,0:T(8,128)S(1)} %bitcast.19, f32[16,128]{1,0:T(8,128)S(1)} %bitcast.21), custom_call_target="tpu_custom_call" | custom-call | tf_op jit(solution)/shard_map/solve/pallas_call | solution.py:192
  37.6 6.2 %all-to-all-start.1 = ((f32[128,1,128]{2,1,0:T(1,128)}), f32[128,1,128]{2,1,0:T(1,128)S(1)}, u32[]{:S(2)}, u32[]{:S(2)}) async-start(f32[128,1,128]{2,1,0:T(1,128)} %bitcast.11), calls=%async_computation.1 | async-start | bytes 131072 | tf_op jit(solution)/shard_map/all_to_all | solution.py:285
  43.8 6.9 %power.1 = bf16[2,1024,2048]{2,1,0:T(8,128)(2,1)} custom-call(bf16[512,128]{1,0:T(8,128)(2,1)S(1)} %bitcast.16, bf16[512,128]{1,0:T(8,128)(2,1)S(1)} %collective-permute-done.other_ref), custom_call_target="tpu_custom_call" | custom-call | flops 536870912 | bytes 9437184 | tf_op jit(solution)/shard_map/power/pallas_call | solution.py:245
  50.7 3.7 %all-to-all-done.1 = f32[128,1,128]{2,1,0:T(1,128)S(1)} async-done(((f32[128,1,128]{2,1,0:T(1,128)}), f32[128,1,128]{2,1,0:T(1,128)S(1)}, u32[]{:S(2)}, u32[]{:S(2)}) %all-to-all-start.1) | async-done | bytes 65568 | tf_op jit(solution)/shard_map/all_to_all | solution.py:285
  54.3 0.0 copy-start.3
  54.3 0.6 %copy-done.3 = f32[128,1,128]{2,1,0:T(1,128)} copy-done((f32[128,1,128]{2,1,0:T(1,128)}, f32[128,1,128]{2,1,0:T(1,128)S(1)}, u32[]{:S(2)}) %copy-start.3) | copy-done | bytes 65560
  55.0 1.5 %turn.1 = f32[2,1,8,128]{3,2,1,0:T(8,128)} custom-call(f32[128,128]{1,0:T(8,128)} %bitcast.26), custom_call_target="tpu_custom_call" | custom-call | tf_op jit(solution)/shard_map/turn/pallas_call | solution.py:287
Async XLA Ops:
  0.6 1.3 %copy-start = (bf16[1,8,71680]{2,1,0:T(8,128)(2,1)S(1)}, bf16[1,8,71680]{2,1,0:T(8,128)(2,1)}, u32[]{:S(2)}) copy-start(bf16[1,8,71680]{2,1,0:T(8,128)(2,1)} %param.5) | copy-start | bytes 3440644
  1.9 1.0 %copy-start.1 = (bf16[256,768]{1,0:T(8,128)(2,1)S(1)}, bf16[256,768]{1,0:T(8,128)(2,1)}, u32[]{:S(2)}) copy-start(bf16[256,768]{1,0:T(8,128)(2,1)} %constant.7.clone.table_ref) | copy-start | bytes 1179652
  2.9 0.8 %copy-start.2 = (f32[8,4,256]{2,1,0:T(4,128)S(1)}, f32[8,4,256]{2,1,0:T(4,128)}, u32[]{:S(2)}) copy-start(f32[8,4,256]{2,1,0:T(4,128)} %constant.6.clone.window_ref) | copy-start | bytes 98308
  31.9 3.6 %collective-permute-start = (bf16[512,128]{1,0:T(8,128)(2,1)S(1)}, bf16[512,128]{1,0:T(8,128)(2,1)S(1)}, u32[]{:S(2)}, u32[]{:S(2)}) collective-permute-start(bf16[512,128]{1,0:T(8,128)(2,1)S(1)} %bitcast.14), channel_id=1, source_target_pairs={{0,1},{1,0},{2,3},{3,2},{4,5},{5,4},{6,7},{7,6},{8,9},{9,8},{10,11... | collective-permute-start | bytes 393224 | tf_op jit(solution)/shard_map/ppermute | solution.py:276
  37.6 16.8 %all-to-all-start.1 = ((f32[128,1,128]{2,1,0:T(1,128)}), f32[128,1,128]{2,1,0:T(1,128)S(1)}, u32[]{:S(2)}, u32[]{:S(2)}) async-start(f32[128,1,128]{2,1,0:T(1,128)} %bitcast.11), calls=%async_computation.1 | async-start | bytes 131072 | tf_op jit(solution)/shard_map/all_to_all | solution.py:285
  54.3 0.6 %copy-start.3 = (f32[128,1,128]{2,1,0:T(1,128)}, f32[128,1,128]{2,1,0:T(1,128)S(1)}, u32[]{:S(2)}) copy-start(f32[128,1,128]{2,1,0:T(1,128)S(1)} %all-to-all-done.1) | copy-start | bytes 196612

commit v2 on v1

--- a/solution.py
+++ b/solution.py
@@ -45,34 +45,59 @@
     scale = 1.0 / math.sqrt(NFFT)
     table = np.concatenate([np.cos(angle), -np.sin(angle)], axis=0) * scale
     high, low = split_bf16(table)
-    return np.concatenate([high, high, low], axis=1)
-
-
-def channelize_kernel(volts_ref, window_ref, table_ref, out_ref, folded_ref, rows_ref):
-    for part in range(FOLD // 128):
-
-        def fold_step(fold, sums):
-            start = pl.multiple_of(fold * FOLD + part * 128, 128)
-            taps = [
-                jnp.broadcast_to(
-                    window_ref[fold, tap : tap + 1, part * 128 : part * 128 + 128],
-                    (OWNED, 128),
-                )
-                for tap in range(TAPS)
-            ]
-            sums = list(sums)
-            for frame in range(SPECTRA + TAPS - 1):
-                piece = volts_ref[:, pl.ds(start + frame * NFFT, 128)].astype(F32)
-                for tap in range(TAPS):
-                    s = frame - tap
-                    if 0 <= s < SPECTRA:
-                        sums[s] = sums[s] + piece * taps[tap]
-            return tuple(sums)
-
-        zero = jnp.zeros((OWNED, 128), F32)
-        sums = lax.fori_loop(0, FOLDS, fold_step, (zero,) * SPECTRA)
-        for s in range(SPECTRA):
-            folded_ref[part, pl.ds(s * OWNED, OWNED), :] = sums[s]
+    return np.concatenate([high, low], axis=1)
+
+
+GROUP = 8
+GROUPS = SPECTRA // GROUP
+
+
+def channelize_kernel(
+    volts_hbm, window_hbm, table_hbm, out_ref,
+    volts_ref, window_ref, table_ref, folded_ref, rows_ref, sems,
+):
+    def frames_copy(group):
+        first = 0 if group == 0 else group * GROUP + TAPS - 1
+        last = (group + 1) * GROUP + TAPS - 1
+        span = pl.ds(first * NFFT, (last - first) * NFFT)
+        return pltpu.make_async_copy(
+            volts_hbm.at[:, span], volts_ref.at[:, span], sems.at[group]
+        )
+
+    window_copy = pltpu.make_async_copy(window_hbm, window_ref, sems.at[GROUPS])
+    table_copy = pltpu.make_async_copy(table_hbm, table_ref, sems.at[GROUPS + 1])
+    window_copy.start()
+    for group in range(GROUPS):
+        frames_copy(group).start()
+    table_copy.start()
+    window_copy.wait()
+    for group in range(GROUPS):
+        frames_copy(group).wait()
+        for part in range(FOLD // 128):
+
+            def fold_step(fold, sums):
+                start = pl.multiple_of(fold * FOLD + part * 128, 128)
+                taps = [
+                    jnp.broadcast_to(
+                        window_ref[fold, tap : tap + 1, part * 128 : part * 128 + 128],
+                        (OWNED, 128),
+                    )
+                    for tap in range(TAPS)
+                ]
+                sums = list(sums)
+                for frame in range(GROUP + TAPS - 1):
+                    offset = start + (group * GROUP + frame) * NFFT
+                    piece = volts_ref[:, pl.ds(offset, 128)].astype(F32)
+                    for tap in range(TAPS):
+                        s = frame - tap
+                        if 0 <= s < GROUP:
+                            sums[s] = sums[s] + piece * taps[tap]
+                return tuple(sums)
+
+            zero = jnp.zeros((OWNED, 128), F32)
+            sums = lax.fori_loop(0, FOLDS, fold_step, (zero,) * GROUP, unroll=2)
+            for s in range(GROUP):
+                folded_ref[part, pl.ds((group * GROUP + s) * OWNED, OWNED), :] = sums[s]
     pieces = []
     for part in range(FOLD // 128):
         pieces.append(
@@ -84,9 +109,14 @@
     folded = jnp.concatenate(pieces, axis=1)
     high = folded.astype(BF16)
     low = (folded - high.astype(F32)).astype(BF16)
-    right = jnp.concatenate([high, low, high], axis=1)
-    spectra = lax.dot_general(
-        table_ref[...], right, (((1,), (1,)), ((), ())), preferred_element_type=F32
+    table_copy.wait()
+    across = (((1,), (1,)), ((), ()))
+    spectra = (
+        lax.dot_general(table_ref[:, 0:FOLD], high, across, preferred_element_type=F32)
+        + lax.dot_general(table_ref[:, 0:FOLD], low, across, preferred_element_type=F32)
+        + lax.dot_general(
+            table_ref[:, FOLD : 2 * FOLD], high, across, preferred_element_type=F32
+        )
     )
     for part in range(2):
         for side in range(2):
@@ -100,30 +130,57 @@
     return pl.pallas_call(
         channelize_kernel,
         out_shape=jax.ShapeDtypeStruct((CHANNELS * 4, 128), BF16),
+        in_specs=[pl.BlockSpec(memory_space=pltpu.HBM)] * 3,
         scratch_shapes=[
+            pltpu.VMEM(volts.shape, BF16),
+            pltpu.VMEM((FOLDS, TAPS, FOLD), F32),
+            pltpu.VMEM((2 * CHANNELS, 2 * FOLD), BF16),
             pltpu.VMEM((2, SPECTRA * OWNED, 128), F32),
             pltpu.VMEM((CHANNELS * 4, 128), F32),
+            pltpu.SemaphoreType.DMA((GROUPS + 2,)),
         ],
-        compiler_params=pltpu.CompilerParams(vmem_limit_bytes=16 * 2**20),
+        compiler_params=pltpu.CompilerParams(vmem_limit_bytes=58 * 2**20),
         name="channelize",
     )(volts, jnp.asarray(fold_weights()), jnp.asarray(transform_weights()))
 
 
+def turn_spectra(source, wide_ref, real_ref, imag_ref):
+    wide_ref[...] = source[...].astype(F32)
+    for part, target in ((0, real_ref), (1, imag_ref)):
+        for group in range(2):
+            block = wide_ref[pl.ds(part * 2 + group, 128, 4), :].T
+            for j in range(4):
+                target[group * 4 + j] = block[j * 32 : j * 32 + 32, :]
+
+
+def own_kernel(own_ref, real_ref, imag_ref, wide_ref):
+    turn_spectra(own_ref, wide_ref, real_ref, imag_ref)
+
+
+def own_turn(own):
+    return pl.pallas_call(
+        own_kernel,
+        out_shape=[jax.ShapeDtypeStruct((OWNED, SPECTRA, 128), F32)] * 2,
+        scratch_shapes=[pltpu.VMEM((512, 128), F32)],
+        compiler_params=pltpu.CompilerParams(vmem_limit_bytes=4 * 2**20),
+        cost_estimate=pl.CostEstimate(
+            flops=2**22, bytes_accessed=2**20, transcendentals=0
+        ),
+        name="own_turn",
+    )(own)
+
+
 def solve_kernel(
-    own_ref, other_ref, mreal_ref, mimag_ref, inverse_ref, out_ref,
-    wide_ref, xr_ref, xi_ref, probe_ref, part_ref,
+    ownr_ref, owni_ref, other_ref, mreal_ref, mimag_ref, inverse_ref, out_ref,
+    wide_ref, otherr_ref, otheri_ref, probe_ref, part_ref,
 ):
-    half = lax.axis_index("bl")
-    for side, source in ((0, own_ref), (1, other_ref)):
-        tile = half if side == 0 else 1 - half
-        wide_ref[...] = source[...].astype(F32)
-        for part in range(2):
-            target = xr_ref if part == 0 else xi_ref
-            for group in range(2):
-                block = wide_ref[pl.ds(part * 2 + group, 128, 4), :].T
-                for j in range(4):
-                    target[tile * OWNED + group * 4 + j] = block[j * 32 : j * 32 + 32, :]
+    turn_spectra(other_ref, wide_ref, otherr_ref, otheri_ref)
     tiles = 2 * OWNED
+
+    def spectra_of(tile):
+        if tile < OWNED:
+            return ownr_ref[tile], owni_ref[tile]
+        return otherr_ref[tile - OWNED], otheri_ref[tile - OWNED]
 
     def gathered(which):
         total = part_ref[which, pl.ds(0, tiles, 8), :]
@@ -135,7 +192,7 @@
         return (values[0:8] + values[8:16]) + (values[16:24] + values[24:32])
 
     for tile in range(tiles):
-        real, imag = xr_ref[tile], xi_ref[tile]
+        real, imag = spectra_of(tile)
         part_ref[0, tile * 8 : tile * 8 + 8, :] = eight(real * real + imag * imag)
     diagonal = gathered(0) * (1.0 / SPECTRA)
     mreal, mimag, inverse = mreal_ref[...], mimag_ref[...], inverse_ref[...]
@@ -150,7 +207,7 @@
         areal = jnp.zeros((SPECTRA, 128), F32)
         aimag = jnp.zeros((SPECTRA, 128), F32)
         for tile in range(tiles):
-            real, imag = xr_ref[tile], xi_ref[tile]
+            real, imag = spectra_of(tile)
             pr = jnp.broadcast_to(probe_ref[0, tile : tile + 1, :], (SPECTRA, 128))
             pi = jnp.broadcast_to(probe_ref[1, tile : tile + 1, :], (SPECTRA, 128))
             areal = areal + (real * pr + imag * pi)
@@ -158,7 +215,7 @@
         sreal = jnp.broadcast_to(jnp.sum(areal, axis=1, keepdims=True), (SPECTRA, 128))
         simag = jnp.broadcast_to(jnp.sum(aimag, axis=1, keepdims=True), (SPECTRA, 128))
         for tile in range(tiles):
-            real, imag = xr_ref[tile], xi_ref[tile]
+            real, imag = spectra_of(tile)
             rows = slice(tile * 8, tile * 8 + 8)
             part_ref[0, rows, :] = eight(real * sreal - imag * simag)
             part_ref[1, rows, :] = eight(real * simag + imag * sreal)
@@ -178,30 +235,27 @@
         return tuple((a + b) * 0.5 for a, b in zip(fresh, first))
 
     greal, gimag = lax.fori_loop(0, ITERS // 2, double_step, (greal, gimag))
-    probe_ref[0] = greal
-    probe_ref[1] = gimag
-    start = pl.multiple_of(half * OWNED, OWNED)
     wide_ref[0:128, :] = jnp.zeros((128, 128), F32)
-    wide_ref[0:8, :] = probe_ref[0, pl.ds(start, OWNED), :]
-    wide_ref[8:16, :] = probe_ref[1, pl.ds(start, OWNED), :]
+    wide_ref[0:8, :] = greal[0:OWNED, :]
+    wide_ref[8:16, :] = gimag[0:OWNED, :]
     out_ref[...] = wide_ref[0:128, :].T
 
 
-def solve(own, other, mreal, mimag, inverse):
+def solve(ownr, owni, other, mreal, mimag, inverse):
     tiles = 2 * OWNED
     return pl.pallas_call(
         solve_kernel,
         out_shape=jax.ShapeDtypeStruct((128, 128), F32),
         scratch_shapes=[
             pltpu.VMEM((512, 128), F32),
-            pltpu.VMEM((tiles, SPECTRA, 128), F32),
-            pltpu.VMEM((tiles, SPECTRA, 128), F32),
+            pltpu.VMEM((OWNED, SPECTRA, 128), F32),
+            pltpu.VMEM((OWNED, SPECTRA, 128), F32),
             pltpu.VMEM((2, tiles, 128), F32),
             pltpu.VMEM((2, tiles * 8, 128), F32),
         ],
-        compiler_params=pltpu.CompilerParams(vmem_limit_bytes=16 * 2**20),
+        compiler_params=pltpu.CompilerParams(vmem_limit_bytes=8 * 2**20),
         name="solve",
-    )(own, other, mreal, mimag, inverse)
+    )(ownr, owni, other, mreal, mimag, inverse)
 
 
 ROWS = 128
@@ -270,23 +324,30 @@
 
 
 def on_device(voltages, model_magnitude, model_phase):
+    half = lax.axis_index("bl")
     spectra = channelize(voltages[0])
     own = lax.all_to_all(spectra.reshape(CHANNELS, 4, 128), "gx", 0, 0)
+
+    def tiles(values):
+        halves = values.reshape(2, 128, OWNED).transpose(0, 2, 1)
+        flipped = jnp.concatenate([halves[1:], halves[:1]], axis=0)
+        return jnp.where(half == 0, halves, flipped).reshape(2 * OWNED, 128)
+
+    magnitude, phase = tiles(model_magnitude), tiles(model_phase)
+    mreal = magnitude * jnp.cos(phase)
+    mimag = magnitude * jnp.sin(phase)
+    inverse = 1.0 / (magnitude * magnitude)
+    own, mreal, mimag, inverse = lax.optimization_barrier((own, mreal, mimag, inverse))
     own = own.reshape(512, 128)
     other = lax.ppermute(own, "bl", [(0, 1), (1, 0)])
-
-    def tiles(values):
-        return values.reshape(2, 128, OWNED).transpose(0, 2, 1).reshape(2 * OWNED, 128)
-
-    mreal = tiles(model_magnitude * jnp.cos(model_phase))
-    mimag = tiles(model_magnitude * jnp.sin(model_phase))
-    inverse = tiles(1.0 / (model_magnitude * model_magnitude))
-    gains = solve(own, other, mreal, mimag, inverse)
+    ownr, owni = own_turn(own)
+    gains = solve(ownr, owni, other, mreal, mimag, inverse)
     moved = lax.all_to_all(gains.reshape(128, 1, 128), "gx", 0, 0)
     visible = power(own, other)
     gain_output = pl.pallas_call(
         turn_kernel,
         out_shape=jax.ShapeDtypeStruct((2, 1, OWNED, CHANNELS), F32),
+        compiler_params=pltpu.CompilerParams(vmem_limit_bytes=2 * 2**20),
         name="turn",
     )(moved.reshape(128, 128))
     return visible[None], gain_output

time: 56.9 us -> 53.7 us (0.944)
  blocking collectives: 27.1 us -> 0 us
  starting transfers between devices: 8.29 us -> 24.7 us
  waiting for transfers between devices: 3.66 us -> 11.8 us
  local copies, waits for them, and re-layouts: 4.11 us -> 0.84 us
  other arithmetic: 1.01 us -> 2.79 us
  Pallas kernels: 11.6 us -> 12.6 us
    all_to_all x1 -> x0, blocking collectives: 27.1 us -> none  [on_device(): own = lax.all_to_all(spectra.reshape(CHANNELS, 4, 128), 'gx', 0, 0)]
    all_to_all x0 -> x1, starting transfers between devices: none -> 16.3 us  [on_device(): own = lax.all_to_all(spectra.reshape(CHANNELS, 4, 128), 'gx', 0, 0)]
    all_to_all x0 -> x1, waiting for transfers between devices: none -> 7.27 us  [on_device(): own = lax.all_to_all(spectra.reshape(CHANNELS, 4, 128), 'gx', 0, 0)]
    unnamed x8 -> x1, local copies, waits for them, and re-layouts: 3.62 us -> 0.51 us
    unnamed x0 -> x2, other arithmetic: none -> 2.73 us
    pallas_call x1, Pallas kernels: 1.15 us -> 3.07 us  [channelize(): pl.pallas_call(channelize_kernel, out_shape=jax.ShapeDtypeStruct((CHANNEL...]
    mul x1, other arithmetic: 1.01 us -> 0.06 us  [on_device(): mimag = magnitude * jnp.sin(phase)]
    ppermute x1, waiting for transfers between devices: 0.01 us -> 0.87 us  [on_device(): other = lax.ppermute(own, 'bl', [(0, 1), (1, 0)])]
  transfers between devices with their start and end apart: 2 -> 3, of which waited for: 1 -> 3; matrix products, arithmetic and copies ran while one was open for 3% -> 7% of each run, Pallas kernels for 12% -> 13%
where the time goes in v2:
time: 53.7 us; the launch traced here: 53.3 us
  starting transfers between devices  24.7 us (46%)
  Pallas kernels  12.6 us (23%)
  waiting for transfers between devices  11.8 us (22%)
  other arithmetic  2.79 us (5%)
  local copies, waits for them, and re-layouts  0.84 us (2%)
  between operations  0.7 us (1%)
    all_to_all x1, starting transfers between devices, on_device(): own = lax.all_to_all(spectra.reshape(CHANNELS, 4, 128), 'gx', 0, 0)  16.3 us
    all_to_all x1, waiting for transfers between devices, on_device(): own = lax.all_to_all(spectra.reshape(CHANNELS, 4, 128), 'gx', 0, 0)  7.27 us
    pallas_call x1, Pallas kernels, power(): pl.pallas_call(power_kernel, grid=(1024 // ROWS,), in_specs=[pl.BlockSpec...  6.92 us
    all_to_all x1, starting transfers between devices, on_device(): moved = lax.all_to_all(gains.reshape(128, 1, 128), 'gx', 0, 0)  6.16 us
    all_to_all x1, waiting for transfers between devices, on_device(): moved = lax.all_to_all(gains.reshape(128, 1, 128), 'gx', 0, 0)  3.65 us
    pallas_call x1, Pallas kernels, channelize(): pl.pallas_call(channelize_kernel, out_shape=jax.ShapeDtypeStruct((CHANNEL...  3.07 us
    unnamed x2, other arithmetic  2.73 us
    ppermute x1, starting transfers between devices, on_device(): other = lax.ppermute(own, 'bl', [(0, 1), (1, 0)])  2.15 us
  transfers between devices with their start and end apart: 3, of which 3 were waited for; matrix products, arithmetic and copies ran while one was open for 7% of the time, Pallas kernels for 13%

profile of v2, /device:TPU:1, one launch (start us, length us, event | category | flops | bytes accessed | tf_op | source)
XLA Modules:
  0.0 53.3 jit_solution(2672944781669664640)
XLA Ops:
  0.6 3.1 %channelize.1 = bf16[512,128]{1,0:T(8,128)(2,1)} custom-call(bf16[8,71680]{1,0:T(8,128)(2,1)} %bitcast.30, f32[8,4,256]{2,1,0:T(4,128)} %constant.12.clone.window_hbm, bf16[256,512]{1,0:T(8,128)(2,1)} %constant.13.clone.table_hbm), custom_call_target="tpu_custom_call" | custom-call | tf_op jit(solution)/shard_map/channelize/pallas_call | solution.py:130
  3.7 16.3 %all-to-all-start = ((bf16[128,4,128]{2,1,0:T(4,128)(2,1)}), bf16[128,4,128]{2,1,0:T(4,128)(2,1)S(1)}, u32[]{:S(2)}, u32[]{:S(2)}) async-start(bf16[128,4,128]{2,1,0:T(4,128)(2,1)} %bitcast.31), calls=%async_computation | async-start | bytes 262144 | tf_op jit(solution)/shard_map/all_to_all | solution.py:329
  20.1 0.5 broadcast.8
  20.6 1.4 %reduce.7 = f32[2048]{0:T(1024)S(1)} reduce(f32[1,2048]{1,0:T(1,128)} %param.6, f32[]{:T(128)} %broadcast.8), dimensions={0}, to_apply=%param.6.reduce_sub_computation.3 | reduce | bytes 16388 | tf_op args[1]
  21.9 1.4 %reduce.6 = f32[2048]{0:T(1024)S(1)} reduce(f32[1,2048]{1,0:T(1,128)} %param.7, f32[]{:T(128)} %broadcast.8), dimensions={0}, to_apply=%param.7.reduce_sub_computation.3 | reduce | bytes 16388 | tf_op args[2]
  23.3 0.1 reshape.33
  23.4 0.1 copy.27
  23.5 0.1 reshape.32
  23.6 0.1 copy.26
  23.7 0.1 multiply_bitcast_fusion
  23.7 7.3 %all-to-all-done = bf16[128,4,128]{2,1,0:T(4,128)(2,1)S(1)} async-done(((bf16[128,4,128]{2,1,0:T(4,128)(2,1)}), bf16[128,4,128]{2,1,0:T(4,128)(2,1)S(1)}, u32[]{:S(2)}, u32[]{:S(2)}) %all-to-all-start) | async-done | bytes 131104 | tf_op jit(solution)/shard_map/all_to_all | solution.py:329
  31.0 2.2 %collective-permute-start = (bf16[512,128]{1,0:T(8,128)(2,1)S(1)}, bf16[512,128]{1,0:T(8,128)(2,1)S(1)}, u32[]{:S(2)}, u32[]{:S(2)}) collective-permute-start(bf16[512,128]{1,0:T(8,128)(2,1)S(1)} %bitcast.25), channel_id=1, source_target_pairs={{0,1},{1,0},{2,3},{3,2},{4,5},{5,4},{6,7},{7,6},{8,9},{9,8},{10,11... | collective-permute-start | bytes 393224 | tf_op jit(solution)/shard_map/ppermute | solution.py:342
  33.2 0.1 own_turn.1
  33.3 0.9 %collective-permute-done.other_ref = bf16[512,128]{1,0:T(8,128)(2,1)S(1)} collective-permute-done((bf16[512,128]{1,0:T(8,128)(2,1)S(1)}, bf16[512,128]{1,0:T(8,128)(2,1)S(1)}, u32[]{:S(2)}, u32[]{:S(2)}) %collective-permute-start) | collective-permute-done | bytes 131104 | tf_op jit(solution)/shard_map/ppermute | solution.py:342
  34.1 1.8 %solve.1 = f32[128,128]{1,0:T(8,128)} custom-call(f32[8,32,128]{2,1,0:T(8,128)S(1)} %get-tuple-element.9.ownr_ref, f32[8,32,128]{2,1,0:T(8,128)S(1)} %get-tuple-element.10.owni_ref, bf16[512,128]{1,0:T(8,128)(2,1)S(1)} %collective-permute-done.other_ref, f32[16,128]{1,0:T(8,128)S(1)} %get-tuple-element.11.mreal_ref, ...), custom_call_target="tpu_custom_call" | custom-call | tf_op jit(solution)/shard_map/solve/pallas_call | solution.py:246
  35.9 6.2 %all-to-all-start.1 = ((f32[128,1,128]{2,1,0:T(1,128)}), f32[128,1,128]{2,1,0:T(1,128)S(1)}, u32[]{:S(2)}, u32[]{:S(2)}) async-start(f32[128,1,128]{2,1,0:T(1,128)} %bitcast.10), calls=%async_computation.1 | async-start | bytes 131072 | tf_op jit(solution)/shard_map/all_to_all | solution.py:345
  42.1 6.9 %power.1 = bf16[2,1024,2048]{2,1,0:T(8,128)(2,1)} custom-call(bf16[512,128]{1,0:T(8,128)(2,1)S(1)} %bitcast.27, bf16[512,128]{1,0:T(8,128)(2,1)S(1)} %collective-permute-done.other_ref), custom_call_target="tpu_custom_call" | custom-call | flops 536870912 | bytes 9437184 | tf_op jit(solution)/shard_map/power/pallas_call | solution.py:299
  49.0 3.7 %all-to-all-done.1 = f32[128,1,128]{2,1,0:T(1,128)S(1)} async-done(((f32[128,1,128]{2,1,0:T(1,128)}), f32[128,1,128]{2,1,0:T(1,128)S(1)}, u32[]{:S(2)}, u32[]{:S(2)}) %all-to-all-start.1) | async-done | bytes 65568 | tf_op jit(solution)/shard_map/all_to_all | solution.py:345
  52.7 0.7 %turn.1 = f32[2,1,8,128]{3,2,1,0:T(8,128)} custom-call(f32[128,128]{1,0:T(8,128)S(1)} %bitcast.28), custom_call_target="tpu_custom_call" | custom-call | tf_op jit(solution)/shard_map/turn/pallas_call | solution.py:347
  (1 shorter events, 0.0 us)
Async XLA Ops:
  3.7 27.3 %all-to-all-start = ((bf16[128,4,128]{2,1,0:T(4,128)(2,1)}), bf16[128,4,128]{2,1,0:T(4,128)(2,1)S(1)}, u32[]{:S(2)}, u32[]{:S(2)}) async-start(bf16[128,4,128]{2,1,0:T(4,128)(2,1)} %bitcast.31), calls=%async_computation | async-start | bytes 262144 | tf_op jit(solution)/shard_map/all_to_all | solution.py:329
  31.0 3.1 %collective-permute-start = (bf16[512,128]{1,0:T(8,128)(2,1)S(1)}, bf16[512,128]{1,0:T(8,128)(2,1)S(1)}, u32[]{:S(2)}, u32[]{:S(2)}) collective-permute-start(bf16[512,128]{1,0:T(8,128)(2,1)S(1)} %bitcast.25), channel_id=1, source_target_pairs={{0,1},{1,0},{2,3},{3,2},{4,5},{5,4},{6,7},{7,6},{8,9},{9,8},{10,11... | collective-permute-start | bytes 393224 | tf_op jit(solution)/shard_map/ppermute | solution.py:342
  35.9 16.7 %all-to-all-start.1 = ((f32[128,1,128]{2,1,0:T(1,128)}), f32[128,1,128]{2,1,0:T(1,128)S(1)}, u32[]{:S(2)}, u32[]{:S(2)}) async-start(f32[128,1,128]{2,1,0:T(1,128)} %bitcast.10), calls=%async_computation.1 | async-start | bytes 131072 | tf_op jit(solution)/shard_map/all_to_all | solution.py:345

commit v3 on v2

--- a/solution.py
+++ b/solution.py
@@ -129,7 +129,7 @@
 def channelize(volts):
     return pl.pallas_call(
         channelize_kernel,
-        out_shape=jax.ShapeDtypeStruct((CHANNELS * 4, 128), BF16),
+        out_shape=pltpu.VMEM((CHANNELS * 4, 128), BF16),
         in_specs=[pl.BlockSpec(memory_space=pltpu.HBM)] * 3,
         scratch_shapes=[
             pltpu.VMEM(volts.shape, BF16),
@@ -139,9 +139,14 @@
             pltpu.VMEM((CHANNELS * 4, 128), F32),
             pltpu.SemaphoreType.DMA((GROUPS + 2,)),
         ],
-        compiler_params=pltpu.CompilerParams(vmem_limit_bytes=58 * 2**20),
+        compiler_params=pltpu.CompilerParams(vmem_limit_bytes=8 * 2**20),
         name="channelize",
-    )(volts, jnp.asarray(fold_weights()), jnp.asarray(transform_weights()))
+    )(*[
+        pltpu.with_memory_space_constraint(operand, pltpu.HBM)
+        for operand in (
+            volts, jnp.asarray(fold_weights()), jnp.asarray(transform_weights())
+        )
+    ])
 
 
 def turn_spectra(source, wide_ref, real_ref, imag_ref):
@@ -245,7 +250,7 @@
     tiles = 2 * OWNED
     return pl.pallas_call(
         solve_kernel,
-        out_shape=jax.ShapeDtypeStruct((128, 128), F32),
+        out_shape=pltpu.VMEM((128, 128), F32),
         scratch_shapes=[
             pltpu.VMEM((512, 128), F32),
             pltpu.VMEM((OWNED, SPECTRA, 128), F32),

time: 53.7 us -> 53.7 us (level)
  no operation moved by 1% of the time
where the time goes in v3:
time: 53.7 us; the launch traced here: 53.3 us
  starting transfers between devices  24.7 us (46%)
  Pallas kernels  12.6 us (23%)
  waiting for transfers between devices  11.8 us (22%)
  other arithmetic  2.79 us (5%)
  local copies, waits for them, and re-layouts  0.84 us (2%)
  between operations  0.7 us (1%)
    all_to_all x1, starting transfers between devices, on_device(): own = lax.all_to_all(spectra.reshape(CHANNELS, 4, 128), 'gx', 0, 0)  16.3 us
    all_to_all x1, waiting for transfers between devices, on_device(): own = lax.all_to_all(spectra.reshape(CHANNELS, 4, 128), 'gx', 0, 0)  7.27 us
    pallas_call x1, Pallas kernels, power(): pl.pallas_call(power_kernel, grid=(1024 // ROWS,), in_specs=[pl.BlockSpec...  6.92 us
    all_to_all x1, starting transfers between devices, on_device(): moved = lax.all_to_all(gains.reshape(128, 1, 128), 'gx', 0, 0)  6.16 us
    all_to_all x1, waiting for transfers between devices, on_device(): moved = lax.all_to_all(gains.reshape(128, 1, 128), 'gx', 0, 0)  3.65 us
    pallas_call x1, Pallas kernels, channelize(): pl.pallas_call(channelize_kernel, out_shape=pltpu.VMEM((CHANNELS * 4, 128...  3.07 us
    unnamed x2, other arithmetic  2.73 us
    ppermute x1, starting transfers between devices, on_device(): other = lax.ppermute(own, 'bl', [(0, 1), (1, 0)])  2.15 us
  transfers between devices with their start and end apart: 3, of which 3 were waited for; matrix products, arithmetic and copies ran while one was open for 7% of the time, Pallas kernels for 13%

profile of v3, /device:TPU:1, one launch (start us, length us, event | category | flops | bytes accessed | tf_op | source)
XLA Modules:
  0.0 53.3 jit_solution(9701714994814041260)
XLA Ops:
  0.6 3.1 %channelize.1 = bf16[512,128]{1,0:T(8,128)(2,1)} custom-call(bf16[8,71680]{1,0:T(8,128)(2,1)} %bitcast.30, f32[8,4,256]{2,1,0:T(4,128)} %constant.12.clone.window_hbm, bf16[256,512]{1,0:T(8,128)(2,1)} %constant.13.clone.table_hbm), custom_call_target="tpu_custom_call" | custom-call | tf_op jit(solution)/shard_map/channelize/pallas_call | solution.py:130
  3.7 16.3 %all-to-all-start = ((bf16[128,4,128]{2,1,0:T(4,128)(2,1)}), bf16[128,4,128]{2,1,0:T(4,128)(2,1)S(1)}, u32[]{:S(2)}, u32[]{:S(2)}) async-start(bf16[128,4,128]{2,1,0:T(4,128)(2,1)} %bitcast.1), calls=%async_computation | async-start | bytes 262144 | tf_op jit(solution)/shard_map/all_to_all | solution.py:334
  20.1 0.5 broadcast.8
  20.6 1.4 %reduce.7 = f32[2048]{0:T(1024)S(1)} reduce(f32[1,2048]{1,0:T(1,128)} %param.6, f32[]{:T(128)} %broadcast.8), dimensions={0}, to_apply=%param.6.reduce_sub_computation.3 | reduce | bytes 16388 | tf_op args[1]
  21.9 1.4 %reduce.6 = f32[2048]{0:T(1024)S(1)} reduce(f32[1,2048]{1,0:T(1,128)} %param.7, f32[]{:T(128)} %broadcast.8), dimensions={0}, to_apply=%param.7.reduce_sub_computation.3 | reduce | bytes 16388 | tf_op args[2]
  23.3 0.1 reshape.33
  23.4 0.1 copy.27
  23.5 0.1 reshape.32
  23.6 0.1 copy.26
  23.7 0.1 multiply_bitcast_fusion
  23.7 7.3 %all-to-all-done = bf16[128,4,128]{2,1,0:T(4,128)(2,1)S(1)} async-done(((bf16[128,4,128]{2,1,0:T(4,128)(2,1)}), bf16[128,4,128]{2,1,0:T(4,128)(2,1)S(1)}, u32[]{:S(2)}, u32[]{:S(2)}) %all-to-all-start) | async-done | bytes 131104 | tf_op jit(solution)/shard_map/all_to_all | solution.py:334
  31.0 2.2 %collective-permute-start = (bf16[512,128]{1,0:T(8,128)(2,1)S(1)}, bf16[512,128]{1,0:T(8,128)(2,1)S(1)}, u32[]{:S(2)}, u32[]{:S(2)}) collective-permute-start(bf16[512,128]{1,0:T(8,128)(2,1)S(1)} %bitcast.25), channel_id=1, source_target_pairs={{0,1},{1,0},{2,3},{3,2},{4,5},{5,4},{6,7},{7,6},{8,9},{9,8},{10,11... | collective-permute-start | bytes 393224 | tf_op jit(solution)/shard_map/ppermute | solution.py:347
  33.2 0.1 own_turn.1
  33.3 0.9 %collective-permute-done.other_ref = bf16[512,128]{1,0:T(8,128)(2,1)S(1)} collective-permute-done((bf16[512,128]{1,0:T(8,128)(2,1)S(1)}, bf16[512,128]{1,0:T(8,128)(2,1)S(1)}, u32[]{:S(2)}, u32[]{:S(2)}) %collective-permute-start) | collective-permute-done | bytes 131104 | tf_op jit(solution)/shard_map/ppermute | solution.py:347
  34.1 1.8 %solve.1 = f32[128,128]{1,0:T(8,128)} custom-call(f32[8,32,128]{2,1,0:T(8,128)S(1)} %get-tuple-element.9.ownr_ref, f32[8,32,128]{2,1,0:T(8,128)S(1)} %get-tuple-element.10.owni_ref, bf16[512,128]{1,0:T(8,128)(2,1)S(1)} %collective-permute-done.other_ref, f32[16,128]{1,0:T(8,128)S(1)} %get-tuple-element.11.mreal_ref, ...), custom_call_target="tpu_custom_call" | custom-call | tf_op jit(solution)/shard_map/solve/pallas_call | solution.py:251
  35.9 6.2 %all-to-all-start.1 = ((f32[128,1,128]{2,1,0:T(1,128)}), f32[128,1,128]{2,1,0:T(1,128)S(1)}, u32[]{:S(2)}, u32[]{:S(2)}) async-start(f32[128,1,128]{2,1,0:T(1,128)} %bitcast.10), calls=%async_computation.1 | async-start | bytes 131072 | tf_op jit(solution)/shard_map/all_to_all | solution.py:350
  42.1 6.9 %power.1 = bf16[2,1024,2048]{2,1,0:T(8,128)(2,1)} custom-call(bf16[512,128]{1,0:T(8,128)(2,1)S(1)} %bitcast.27, bf16[512,128]{1,0:T(8,128)(2,1)S(1)} %collective-permute-done.other_ref), custom_call_target="tpu_custom_call" | custom-call | flops 536870912 | bytes 9437184 | tf_op jit(solution)/shard_map/power/pallas_call | solution.py:304
  49.0 3.7 %all-to-all-done.1 = f32[128,1,128]{2,1,0:T(1,128)S(1)} async-done(((f32[128,1,128]{2,1,0:T(1,128)}), f32[128,1,128]{2,1,0:T(1,128)S(1)}, u32[]{:S(2)}, u32[]{:S(2)}) %all-to-all-start.1) | async-done | bytes 65568 | tf_op jit(solution)/shard_map/all_to_all | solution.py:350
  52.7 0.7 %turn.1 = f32[2,1,8,128]{3,2,1,0:T(8,128)} custom-call(f32[128,128]{1,0:T(8,128)S(1)} %bitcast.28), custom_call_target="tpu_custom_call" | custom-call | tf_op jit(solution)/shard_map/turn/pallas_call | solution.py:352
  (1 shorter events, 0.0 us)
Async XLA Ops:
  3.7 27.3 %all-to-all-start = ((bf16[128,4,128]{2,1,0:T(4,128)(2,1)}), bf16[128,4,128]{2,1,0:T(4,128)(2,1)S(1)}, u32[]{:S(2)}, u32[]{:S(2)}) async-start(bf16[128,4,128]{2,1,0:T(4,128)(2,1)} %bitcast.1), calls=%async_computation | async-start | bytes 262144 | tf_op jit(solution)/shard_map/all_to_all | solution.py:334
  31.0 3.1 %collective-permute-start = (bf16[512,128]{1,0:T(8,128)(2,1)S(1)}, bf16[512,128]{1,0:T(8,128)(2,1)S(1)}, u32[]{:S(2)}, u32[]{:S(2)}) collective-permute-start(bf16[512,128]{1,0:T(8,128)(2,1)S(1)} %bitcast.25), channel_id=1, source_target_pairs={{0,1},{1,0},{2,3},{3,2},{4,5},{5,4},{6,7},{7,6},{8,9},{9,8},{10,11... | collective-permute-start | bytes 393224 | tf_op jit(solution)/shard_map/ppermute | solution.py:347
  35.9 16.7 %all-to-all-start.1 = ((f32[128,1,128]{2,1,0:T(1,128)}), f32[128,1,128]{2,1,0:T(1,128)S(1)}, u32[]{:S(2)}, u32[]{:S(2)}) async-start(f32[128,1,128]{2,1,0:T(1,128)} %bitcast.10), calls=%async_computation.1 | async-start | bytes 131072 | tf_op jit(solution)/shard_map/all_to_all | solution.py:350

commit v4 on v2

--- a/solution.py
+++ b/solution.py
@@ -50,54 +50,71 @@
 
 GROUP = 8
 GROUPS = SPECTRA // GROUP
+TILES = 2 * OWNED
 
 
 def channelize_kernel(
-    volts_hbm, window_hbm, table_hbm, out_ref,
-    volts_ref, window_ref, table_ref, folded_ref, rows_ref, sems,
+    volts_hbm, window_hbm, table_hbm, magnitude_hbm, phase_hbm, out_ref, model_ref,
+    volts_ref, window_ref, table_ref, magnitude_ref, phase_ref, folded_ref, rows_ref, sems,
 ):
-    def frames_copy(group):
-        first = 0 if group == 0 else group * GROUP + TAPS - 1
-        last = (group + 1) * GROUP + TAPS - 1
-        span = pl.ds(first * NFFT, (last - first) * NFFT)
+    def frames_copy(first, count, slot):
+        start = first * NFFT
+        if not isinstance(first, int):
+            start = pl.multiple_of(start, NFFT)
+        span = pl.ds(start, count * NFFT)
         return pltpu.make_async_copy(
-            volts_hbm.at[:, span], volts_ref.at[:, span], sems.at[group]
+            volts_hbm.at[:, span], volts_ref.at[:, span], sems.at[slot]
         )
 
-    window_copy = pltpu.make_async_copy(window_hbm, window_ref, sems.at[GROUPS])
-    table_copy = pltpu.make_async_copy(table_hbm, table_ref, sems.at[GROUPS + 1])
-    window_copy.start()
+    lead = TAPS - 1
+    copies = [
+        pltpu.make_async_copy(window_hbm, window_ref, sems.at[GROUPS]),
+        frames_copy(0, lead, GROUPS + 1),
+    ]
+    model_copies = [
+        pltpu.make_async_copy(magnitude_hbm, magnitude_ref, sems.at[GROUPS + 2]),
+        pltpu.make_async_copy(phase_hbm, phase_ref, sems.at[GROUPS + 3]),
+    ]
+    table_copy = pltpu.make_async_copy(table_hbm, table_ref, sems.at[GROUPS + 4])
+    for copy in model_copies + copies:
+        copy.start()
     for group in range(GROUPS):
-        frames_copy(group).start()
+        frames_copy(group * GROUP + lead, GROUP, group).start()
     table_copy.start()
-    window_copy.wait()
-    for group in range(GROUPS):
-        frames_copy(group).wait()
+    for copy in model_copies:
+        copy.wait()
+    magnitude, phase = magnitude_ref[...], phase_ref[...]
+    model_ref[0:TILES, :] = magnitude * jnp.cos(phase)
+    model_ref[TILES : 2 * TILES, :] = magnitude * jnp.sin(phase)
+    model_ref[2 * TILES : 3 * TILES, :] = 1.0 / (magnitude * magnitude)
+    for copy in copies:
+        copy.wait()
+
+    def group_step(group, carry):
+        first = group * GROUP
+        frames_copy(first + lead, GROUP, group).wait()
         for part in range(FOLD // 128):
-
-            def fold_step(fold, sums):
-                start = pl.multiple_of(fold * FOLD + part * 128, 128)
+            lanes = slice(part * 128, part * 128 + 128)
+            sums = [jnp.zeros((OWNED, 128), F32)] * GROUP
+            for fold in range(FOLDS):
                 taps = [
-                    jnp.broadcast_to(
-                        window_ref[fold, tap : tap + 1, part * 128 : part * 128 + 128],
-                        (OWNED, 128),
-                    )
+                    jnp.broadcast_to(window_ref[fold, tap : tap + 1, lanes], (OWNED, 128))
                     for tap in range(TAPS)
                 ]
-                sums = list(sums)
                 for frame in range(GROUP + TAPS - 1):
-                    offset = start + (group * GROUP + frame) * NFFT
-                    piece = volts_ref[:, pl.ds(offset, 128)].astype(F32)
+                    offset = (first + frame) * NFFT + fold * FOLD + part * 128
+                    piece = volts_ref[:, pl.ds(pl.multiple_of(offset, 128), 128)]
+                    piece = piece.astype(F32)
                     for tap in range(TAPS):
                         s = frame - tap
                         if 0 <= s < GROUP:
                             sums[s] = sums[s] + piece * taps[tap]
-                return tuple(sums)
-
-            zero = jnp.zeros((OWNED, 128), F32)
-            sums = lax.fori_loop(0, FOLDS, fold_step, (zero,) * GROUP, unroll=2)
             for s in range(GROUP):
-                folded_ref[part, pl.ds((group * GROUP + s) * OWNED, OWNED), :] = sums[s]
+                row = pl.multiple_of((first + s) * OWNED, OWNED)
+                folded_ref[part, pl.ds(row, OWNED), :] = sums[s]
+        return carry
+
+    lax.fori_loop(0, GROUPS, group_step, 0)
     pieces = []
     for part in range(FOLD // 128):
         pieces.append(
@@ -126,22 +143,34 @@
     out_ref[...] = rows_ref[...].astype(BF16)
 
 
-def channelize(volts):
+def channelize(volts, magnitude, phase):
+    operands = (
+        volts,
+        jnp.asarray(fold_weights()),
+        jnp.asarray(transform_weights()),
+        magnitude.reshape(TILES, 128),
+        phase.reshape(TILES, 128),
+    )
     return pl.pallas_call(
         channelize_kernel,
-        out_shape=jax.ShapeDtypeStruct((CHANNELS * 4, 128), BF16),
-        in_specs=[pl.BlockSpec(memory_space=pltpu.HBM)] * 3,
+        out_shape=[
+            pltpu.VMEM((CHANNELS * 4, 128), BF16),
+            pltpu.VMEM((3 * TILES, 128), F32),
+        ],
+        in_specs=[pl.BlockSpec(memory_space=pltpu.HBM)] * 5,
         scratch_shapes=[
             pltpu.VMEM(volts.shape, BF16),
             pltpu.VMEM((FOLDS, TAPS, FOLD), F32),
             pltpu.VMEM((2 * CHANNELS, 2 * FOLD), BF16),
+            pltpu.VMEM((TILES, 128), F32),
+            pltpu.VMEM((TILES, 128), F32),
             pltpu.VMEM((2, SPECTRA * OWNED, 128), F32),
             pltpu.VMEM((CHANNELS * 4, 128), F32),
-            pltpu.SemaphoreType.DMA((GROUPS + 2,)),
+            pltpu.SemaphoreType.DMA((GROUPS + 5,)),
         ],
-        compiler_params=pltpu.CompilerParams(vmem_limit_bytes=58 * 2**20),
+        compiler_params=pltpu.CompilerParams(vmem_limit_bytes=8 * 2**20),
         name="channelize",
-    )(volts, jnp.asarray(fold_weights()), jnp.asarray(transform_weights()))
+    )(*[pltpu.with_memory_space_constraint(x, pltpu.HBM) for x in operands])
 
 
 def turn_spectra(source, wide_ref, real_ref, imag_ref):
@@ -171,7 +200,7 @@
 
 
 def solve_kernel(
-    ownr_ref, owni_ref, other_ref, mreal_ref, mimag_ref, inverse_ref, out_ref,
+    ownr_ref, owni_ref, other_ref, model_ref, out_ref,
     wide_ref, otherr_ref, otheri_ref, probe_ref, part_ref,
 ):
     turn_spectra(other_ref, wide_ref, otherr_ref, otheri_ref)
@@ -195,7 +224,16 @@
         real, imag = spectra_of(tile)
         part_ref[0, tile * 8 : tile * 8 + 8, :] = eight(real * real + imag * imag)
     diagonal = gathered(0) * (1.0 / SPECTRA)
-    mreal, mimag, inverse = mreal_ref[...], mimag_ref[...], inverse_ref[...]
+    half = lax.axis_index("bl")
+
+    def model(which):
+        rows = [
+            pl.ds(pl.multiple_of(which * tiles + side * OWNED, OWNED), OWNED)
+            for side in (half, 1 - half)
+        ]
+        return jnp.concatenate([model_ref[r, :] for r in rows], axis=0)
+
+    mreal, mimag, inverse = model(0), model(1), model(2)
 
     def single_step(greal, gimag):
         yreal = greal * mreal - gimag * mimag
@@ -241,11 +279,11 @@
     out_ref[...] = wide_ref[0:128, :].T
 
 
-def solve(ownr, owni, other, mreal, mimag, inverse):
+def solve(ownr, owni, other, model):
     tiles = 2 * OWNED
     return pl.pallas_call(
         solve_kernel,
-        out_shape=jax.ShapeDtypeStruct((128, 128), F32),
+        out_shape=pltpu.VMEM((128, 128), F32),
         scratch_shapes=[
             pltpu.VMEM((512, 128), F32),
             pltpu.VMEM((OWNED, SPECTRA, 128), F32),
@@ -255,7 +293,7 @@
         ],
         compiler_params=pltpu.CompilerParams(vmem_limit_bytes=8 * 2**20),
         name="solve",
-    )(ownr, owni, other, mreal, mimag, inverse)
+    )(ownr, owni, other, model)
 
 
 ROWS = 128
@@ -324,24 +362,14 @@
 
 
 def on_device(voltages, model_magnitude, model_phase):
-    half = lax.axis_index("bl")
-    spectra = channelize(voltages[0])
+    spectra, model = channelize(voltages[0], model_magnitude, model_phase)
     own = lax.all_to_all(spectra.reshape(CHANNELS, 4, 128), "gx", 0, 0)
-
-    def tiles(values):
-        halves = values.reshape(2, 128, OWNED).transpose(0, 2, 1)
-        flipped = jnp.concatenate([halves[1:], halves[:1]], axis=0)
-        return jnp.where(half == 0, halves, flipped).reshape(2 * OWNED, 128)
-
-    magnitude, phase = tiles(model_magnitude), tiles(model_phase)
-    mreal = magnitude * jnp.cos(phase)
-    mimag = magnitude * jnp.sin(phase)
-    inverse = 1.0 / (magnitude * magnitude)
-    own, mreal, mimag, inverse = lax.optimization_barrier((own, mreal, mimag, inverse))
+    own, model = lax.optimization_barrier((own, model))
     own = own.reshape(512, 128)
     other = lax.ppermute(own, "bl", [(0, 1), (1, 0)])
+    model = model.reshape(6, 128, OWNED).transpose(0, 2, 1).reshape(3 * TILES, 128)
     ownr, owni = own_turn(own)
-    gains = solve(ownr, owni, other, mreal, mimag, inverse)
+    gains = solve(ownr, owni, other, model)
     moved = lax.all_to_all(gains.reshape(128, 1, 128), "gx", 0, 0)
     visible = power(own, other)
     gain_output = pl.pallas_call(

time: 53.7 us -> 52.6 us (0.980)
  blocking collectives: 0 us -> 27.1 us
  starting transfers between devices: 24.7 us -> 8.21 us
  waiting for transfers between devices: 11.8 us -> 4.12 us
  other arithmetic: 2.79 us -> 0 us
  Pallas kernels: 12.6 us -> 11.9 us
    all_to_all x0 -> x1, blocking collectives: none -> 27.1 us  [on_device(): own = lax.all_to_all(spectra.reshape(CHANNELS, 4, 128), 'gx', 0, 0)]
    all_to_all x1 -> x0, starting transfers between devices: 16.3 us -> none  [on_device(): own = lax.all_to_all(spectra.reshape(CHANNELS, 4, 128), 'gx', 0, 0)]
    all_to_all x1 -> x0, waiting for transfers between devices: 7.27 us -> none  [on_device(): own = lax.all_to_all(spectra.reshape(CHANNELS, 4, 128), 'gx', 0, 0)]
    unnamed x2 -> x0, other arithmetic: 2.73 us -> none
    pallas_call x2, Pallas kernels: 4.87 us -> 4.22 us  [the longest x1 2.41 us: channelize(): pl.pallas_call(channelize_kernel, out_shape=[pltpu.VMEM((CHANNELS * 4, 12...]
  transfers between devices with their start and end apart: 3 -> 2, of which waited for: 3 -> 2; matrix products, arithmetic and copies ran while one was open for 7% -> 1% of each run, Pallas kernels for 13% -> 13%
where the time goes in v4:
time: 52.6 us; the launch traced here: 52.4 us
  blocking collectives  27.1 us (52%)
  Pallas kernels  11.9 us (23%)
  starting transfers between devices  8.21 us (16%)
  waiting for transfers between devices  4.12 us (8%)
  between operations  0.67 us (1%)
    all_to_all x1, blocking collectives, on_device(): own = lax.all_to_all(spectra.reshape(CHANNELS, 4, 128), 'gx', 0, 0)  27.1 us
    pallas_call x1, Pallas kernels, power(): pl.pallas_call(power_kernel, grid=(1024 // ROWS,), in_specs=[pl.BlockSpec...  6.92 us
    all_to_all x1, starting transfers between devices, on_device(): moved = lax.all_to_all(gains.reshape(128, 1, 128), 'gx', 0, 0)  6.1 us
    all_to_all x1, waiting for transfers between devices, on_device(): moved = lax.all_to_all(gains.reshape(128, 1, 128), 'gx', 0, 0)  3.62 us
    pallas_call x1, Pallas kernels, channelize(): pl.pallas_call(channelize_kernel, out_shape=[pltpu.VMEM((CHANNELS * 4, 12...  2.41 us
    ppermute x1, starting transfers between devices, on_device(): other = lax.ppermute(own, 'bl', [(0, 1), (1, 0)])  2.12 us
    pallas_call x1, Pallas kernels, solve(): pl.pallas_call(solve_kernel, out_shape=pltpu.VMEM((128, 128), F32), scrat...  1.81 us
  transfers between devices with their start and end apart: 2, of which 2 were waited for; matrix products, arithmetic and copies ran while one was open for 1% of the time, Pallas kernels for 13%

profile of v4, /device:TPU:1, one launch (start us, length us, event | category | flops | bytes accessed | tf_op | source)
XLA Modules:
  0.0 52.4 jit_solution(5192171409234046506)
XLA Ops:
  0.6 2.4 %channelize.1 = (bf16[512,128]{1,0:T(8,128)(2,1)S(1)}, f32[48,128]{1,0:T(8,128)S(1)}) custom-call(bf16[8,71680]{1,0:T(8,128)(2,1)} %bitcast.20, f32[8,4,256]{2,1,0:T(4,128)} %constant.4.clone.window_hbm, bf16[256,512]{1,0:T(8,128)(2,1)} %constant.5.clone.table_hbm, f32[16,128]{1,0:T(8,128)} %bitcast.21, f32[16,128]{1,0:T(8,128)} %bitcast.22), custom_call_target="tpu_custom_call" | custom-call | tf_op jit(solution)/shard_map/channelize/pallas_call | solution.py:154
  3.0 27.1 %all_to_all.10 = bf16[128,4,128]{2,1,0:T(4,128)(2,1)S(1)} all-to-all(bf16[128,4,128]{2,1,0:T(4,128)(2,1)S(1)} %bitcast.16), channel_id=1, replica_groups=mesh['gx'=128,'bl'=2] {'gx'}, dimensions={0} | all-to-all | bytes 262144 | tf_op jit(solution)/shard_map/all_to_all | solution.py:366
  30.2 2.1 %collective-permute-start = (bf16[512,128]{1,0:T(8,128)(2,1)S(1)}, bf16[512,128]{1,0:T(8,128)(2,1)S(1)}, u32[]{:S(2)}, u32[]{:S(2)}) collective-permute-start(bf16[512,128]{1,0:T(8,128)(2,1)S(1)} %bitcast.12), channel_id=1, source_target_pairs={{0,1},{1,0},{2,3},{3,2},{4,5},{5,4},{6,7},{7,6},{8,9},{9,8},{10,11... | collective-permute-start | bytes 393224 | tf_op jit(solution)/shard_map/ppermute | solution.py:369
  32.3 0.2 reshape.32
  32.5 0.1 copy.9
  32.6 0.1 own_turn.1
  32.8 0.5 collective-permute-done.other_ref
  33.3 1.8 %solve.1 = f32[128,128]{1,0:T(8,128)} custom-call(f32[8,32,128]{2,1,0:T(8,128)S(1)} %get-tuple-element.11.ownr_ref, f32[8,32,128]{2,1,0:T(8,128)S(1)} %get-tuple-element.12.owni_ref, bf16[512,128]{1,0:T(8,128)(2,1)S(1)} %collective-permute-done.other_ref, f32[48,128]{1,0:T(8,128)S(1)} %bitcast.17), custom_call_target="tpu_custom_call" | custom-call | tf_op jit(solution)/shard_map/solve/pallas_call | solution.py:284
  35.1 6.1 %all-to-all-start.1 = ((f32[128,1,128]{2,1,0:T(1,128)}), f32[128,1,128]{2,1,0:T(1,128)S(1)}, u32[]{:S(2)}, u32[]{:S(2)}) async-start(f32[128,1,128]{2,1,0:T(1,128)} %bitcast.9), calls=%async_computation.1 | async-start | bytes 131072 | tf_op jit(solution)/shard_map/all_to_all | solution.py:373
  41.2 6.9 %power.1 = bf16[2,1024,2048]{2,1,0:T(8,128)(2,1)} custom-call(bf16[512,128]{1,0:T(8,128)(2,1)S(1)} %bitcast.14, bf16[512,128]{1,0:T(8,128)(2,1)S(1)} %collective-permute-done.other_ref), custom_call_target="tpu_custom_call" | custom-call | flops 536870912 | bytes 9437184 | tf_op jit(solution)/shard_map/power/pallas_call | solution.py:337
  48.1 3.6 %all-to-all-done.1 = f32[128,1,128]{2,1,0:T(1,128)S(1)} async-done(((f32[128,1,128]{2,1,0:T(1,128)}), f32[128,1,128]{2,1,0:T(1,128)S(1)}, u32[]{:S(2)}, u32[]{:S(2)}) %all-to-all-start.1) | async-done | bytes 65568 | tf_op jit(solution)/shard_map/all_to_all | solution.py:373
  51.7 0.7 %turn.1 = f32[2,1,8,128]{3,2,1,0:T(8,128)} custom-call(f32[128,128]{1,0:T(8,128)S(1)} %bitcast.15), custom_call_target="tpu_custom_call" | custom-call | tf_op jit(solution)/shard_map/turn/pallas_call | solution.py:375
Async XLA Ops:
  30.2 3.1 %collective-permute-start = (bf16[512,128]{1,0:T(8,128)(2,1)S(1)}, bf16[512,128]{1,0:T(8,128)(2,1)S(1)}, u32[]{:S(2)}, u32[]{:S(2)}) collective-permute-start(bf16[512,128]{1,0:T(8,128)(2,1)S(1)} %bitcast.12), channel_id=1, source_target_pairs={{0,1},{1,0},{2,3},{3,2},{4,5},{5,4},{6,7},{7,6},{8,9},{9,8},{10,11... | collective-permute-start | bytes 393224 | tf_op jit(solution)/shard_map/ppermute | solution.py:369
  35.1 16.7 %all-to-all-start.1 = ((f32[128,1,128]{2,1,0:T(1,128)}), f32[128,1,128]{2,1,0:T(1,128)S(1)}, u32[]{:S(2)}, u32[]{:S(2)}) async-start(f32[128,1,128]{2,1,0:T(1,128)} %bitcast.9), calls=%async_computation.1 | async-start | bytes 131072 | tf_op jit(solution)/shard_map/all_to_all | solution.py:373

commit v5 on v4

--- a/solution.py
+++ b/solution.py
@@ -22,6 +22,19 @@
 FOLDS = NFFT // FOLD
 
 
+SIDE = 4
+DEPTH = 8
+PLANES = [
+    [(x * DEPTH + z) * SIDE + y for x in range(SIDE) for y in range(SIDE)]
+    for z in range(DEPTH)
+]
+LINES = [
+    [(x * DEPTH + z) * SIDE + y for z in range(DEPTH)]
+    for x in range(SIDE)
+    for y in range(SIDE)
+]
+
+
 def split_bf16(values):
     high = values.astype(np.float32).astype(jnp.bfloat16)
     low = (values - high.astype(np.float64)).astype(np.float32).astype(jnp.bfloat16)
@@ -39,7 +52,7 @@
 
 
 def transform_weights():
-    odd = 2 * np.arange(CHANNELS) + 1
+    odd = 2 * np.array(PLANES).T.reshape(CHANNELS) + 1
     phase = (odd[:, None] * np.arange(FOLD)[None, :]) % (2 * FOLD)
     angle = phase.astype(np.float64) * (2.0 * np.pi / (2 * FOLD))
     scale = 1.0 / math.sqrt(NFFT)
@@ -173,8 +186,15 @@
     )(*[pltpu.with_memory_space_constraint(x, pltpu.HBM) for x in operands])
 
 
+def widen(source, wide_ref):
+    for x in range(SIDE):
+        for z in range(DEPTH):
+            to, at = 16 * (x * DEPTH + z), 16 * (z * SIDE + x)
+            wide_ref[to : to + 16, :] = source[at : at + 16, :].astype(F32)
+
+
 def turn_spectra(source, wide_ref, real_ref, imag_ref):
-    wide_ref[...] = source[...].astype(F32)
+    widen(source, wide_ref)
     for part, target in ((0, real_ref), (1, imag_ref)):
         for group in range(2):
             block = wide_ref[pl.ds(part * 2 + group, 128, 4), :].T
@@ -307,7 +327,7 @@
     def _():
         for side, source in ((0, own_ref), (1, other_ref)):
             tile = half if side == 0 else 1 - half
-            wide_ref[...] = source[...].astype(F32)
+            widen(source, wide_ref)
             for group in range(2):
                 real = wide_ref[pl.ds(group, 128, 4), :]
                 imag = wide_ref[pl.ds(2 + group, 128, 4), :]
@@ -363,7 +383,10 @@
 
 def on_device(voltages, model_magnitude, model_phase):
     spectra, model = channelize(voltages[0], model_magnitude, model_phase)
-    own = lax.all_to_all(spectra.reshape(CHANNELS, 4, 128), "gx", 0, 0)
+    staged = spectra.reshape(SIDE * SIDE, DEPTH, 4, 128)
+    staged = lax.all_to_all(staged, "gx", 0, 0, axis_index_groups=PLANES)
+    staged = staged.transpose(1, 0, 2, 3)
+    own = lax.all_to_all(staged, "gx", 0, 0, axis_index_groups=LINES)
     own, model = lax.optimization_barrier((own, model))
     own = own.reshape(512, 128)
     other = lax.ppermute(own, "bl", [(0, 1), (1, 0)])

time: 52.6 us -> 57 us (1.084)
  blocking collectives: 27.1 us -> 30.3 us
  starting transfers between devices: 8.21 us -> 9.35 us
    all_to_all x1 -> x2, blocking collectives: 27.1 us -> 30.3 us  [the longest x1 16 us: on_device(): own = lax.all_to_all(staged, 'gx', 0, 0, axis_index_groups=LINES)]
    ppermute x1, starting transfers between devices: 2.12 us -> 3.25 us  [on_device(): other = lax.ppermute(own, 'bl', [(0, 1), (1, 0)])]
  transfers between devices with their start and end apart: 2 -> 2, of which waited for: 2 -> 2; matrix products, arithmetic and copies ran while one was open for 1% -> 1% of each run, Pallas kernels for 13% -> 12%
where the time goes in v5:
time: 57 us; the launch traced here: 56.7 us
  blocking collectives  30.3 us (53%)
  Pallas kernels  11.9 us (21%)
  starting transfers between devices  9.35 us (16%)
  waiting for transfers between devices  4.13 us (7%)
  between operations  0.67 us (1%)
    all_to_all x1, blocking collectives, on_device(): own = lax.all_to_all(staged, 'gx', 0, 0, axis_index_groups=LINES)  16 us
    all_to_all x1, blocking collectives, on_device(): staged = lax.all_to_all(staged, 'gx', 0, 0, axis_index_groups=PLANES)  14.2 us
    pallas_call x1, Pallas kernels, power(): pl.pallas_call(power_kernel, grid=(1024 // ROWS,), in_specs=[pl.BlockSpec...  6.92 us
    all_to_all x1, starting transfers between devices, on_device(): moved = lax.all_to_all(gains.reshape(128, 1, 128), 'gx', 0, 0)  6.1 us
    all_to_all x1, waiting for transfers between devices, on_device(): moved = lax.all_to_all(gains.reshape(128, 1, 128), 'gx', 0, 0)  3.63 us
    ppermute x1, starting transfers between devices, on_device(): other = lax.ppermute(own, 'bl', [(0, 1), (1, 0)])  3.25 us
    pallas_call x1, Pallas kernels, channelize(): pl.pallas_call(channelize_kernel, out_shape=[pltpu.VMEM((CHANNELS * 4, 12...  2.41 us
    pallas_call x1, Pallas kernels, solve(): pl.pallas_call(solve_kernel, out_shape=pltpu.VMEM((128, 128), F32), scrat...  1.81 us
  transfers between devices with their start and end apart: 2, of which 2 were waited for; matrix products, arithmetic and copies ran while one was open for 1% of the time, Pallas kernels for 12%

profile of v5, /device:TPU:1, one launch (start us, length us, event | category | flops | bytes accessed | tf_op | source)
XLA Modules:
  0.0 56.7 jit_solution(7173578441534340328)
XLA Ops:
  0.6 2.4 %channelize.1 = (bf16[512,128]{1,0:T(8,128)(2,1)S(1)}, f32[48,128]{1,0:T(8,128)S(1)}) custom-call(bf16[8,71680]{1,0:T(8,128)(2,1)} %bitcast.21, f32[8,4,256]{2,1,0:T(4,128)} %constant.4.clone.window_hbm, bf16[256,512]{1,0:T(8,128)(2,1)} %constant.5.clone.table_hbm, f32[16,128]{1,0:T(8,128)} %bitcast.23, f32[16,128]{1,0:T(8,128)} %bitcast.24), custom_call_target="tpu_custom_call" | custom-call | tf_op jit(solution)/shard_map/channelize/pallas_call | solution.py:167
  3.0 14.2 %all_to_all.15 = bf16[16,8,4,128]{3,2,1,0:T(4,128)(2,1)S(1)} all-to-all(bf16[16,8,4,128]{3,2,1,0:T(4,128)(2,1)S(1)} %bitcast.17), channel_id=1, replica_groups={{0,2,4,6,64,66,68,70,128,130,132,134,192,194,196,198},{8,10,12,14,72,74..., dimensions={0} | all-to-all | bytes 262144 | tf_op jit(solution)/shard_map/all_to_all | solution.py:387
  17.4 16.0 %all_to_all.16 = bf16[8,16,4,128]{3,2,1,0:T(4,128)(2,1)S(1)} all-to-all(bf16[8,16,4,128]{3,2,1,0:T(4,128)(2,1)S(1)} %copy.14), channel_id=1, replica_groups={{0,8,16,24,32,40,48,56},{2,10,18,26,34,42,50,58},{4,12,20,28,36,44,52,6..., dimensions={0} | all-to-all | bytes 262144 | tf_op jit(solution)/shard_map/all_to_all | solution.py:389
  33.4 3.3 %collective-permute-start = (bf16[512,128]{1,0:T(8,128)(2,1)S(1)}, bf16[512,128]{1,0:T(8,128)(2,1)S(1)}, u32[]{:S(2)}, u32[]{:S(2)}) collective-permute-start(bf16[512,128]{1,0:T(8,128)(2,1)S(1)} %bitcast.13), channel_id=1, source_target_pairs={{0,1},{1,0},{2,3},{3,2},{4,5},{5,4},{6,7},{7,6},{8,9},{9,8},{10,11... | collective-permute-start | bytes 393224 | tf_op jit(solution)/shard_map/ppermute | solution.py:392
  36.6 0.2 reshape.32
  36.9 0.1 copy.15
  37.0 0.1 own_turn.1
  37.1 0.5 collective-permute-done.other_ref
  37.6 1.8 %solve.1 = f32[128,128]{1,0:T(8,128)} custom-call(f32[8,32,128]{2,1,0:T(8,128)S(1)} %get-tuple-element.11.ownr_ref, f32[8,32,128]{2,1,0:T(8,128)S(1)} %get-tuple-element.12.owni_ref, bf16[512,128]{1,0:T(8,128)(2,1)S(1)} %collective-permute-done.other_ref, f32[48,128]{1,0:T(8,128)S(1)} %bitcast.18), custom_call_target="tpu_custom_call" | custom-call | tf_op jit(solution)/shard_map/solve/pallas_call | solution.py:304
  39.4 6.1 %all-to-all-start.2 = ((f32[128,1,128]{2,1,0:T(1,128)}), f32[128,1,128]{2,1,0:T(1,128)S(1)}, u32[]{:S(2)}, u32[]{:S(2)}) async-start(f32[128,1,128]{2,1,0:T(1,128)} %bitcast.10), calls=%async_computation.2 | async-start | bytes 131072 | tf_op jit(solution)/shard_map/all_to_all | solution.py:396
  45.5 6.9 %power.1 = bf16[2,1024,2048]{2,1,0:T(8,128)(2,1)} custom-call(bf16[512,128]{1,0:T(8,128)(2,1)S(1)} %bitcast.15, bf16[512,128]{1,0:T(8,128)(2,1)S(1)} %collective-permute-done.other_ref), custom_call_target="tpu_custom_call" | custom-call | flops 536870912 | bytes 9437184 | tf_op jit(solution)/shard_map/power/pallas_call | solution.py:357
  52.4 3.6 %all-to-all-done.2 = f32[128,1,128]{2,1,0:T(1,128)S(1)} async-done(((f32[128,1,128]{2,1,0:T(1,128)}), f32[128,1,128]{2,1,0:T(1,128)S(1)}, u32[]{:S(2)}, u32[]{:S(2)}) %all-to-all-start.2) | async-done | bytes 65568 | tf_op jit(solution)/shard_map/all_to_all | solution.py:396
  56.1 0.7 %turn.1 = f32[2,1,8,128]{3,2,1,0:T(8,128)} custom-call(f32[128,128]{1,0:T(8,128)S(1)} %bitcast.16), custom_call_target="tpu_custom_call" | custom-call | tf_op jit(solution)/shard_map/turn/pallas_call | solution.py:398
  (1 shorter events, 0.0 us)
Async XLA Ops:
  33.4 4.2 %collective-permute-start = (bf16[512,128]{1,0:T(8,128)(2,1)S(1)}, bf16[512,128]{1,0:T(8,128)(2,1)S(1)}, u32[]{:S(2)}, u32[]{:S(2)}) collective-permute-start(bf16[512,128]{1,0:T(8,128)(2,1)S(1)} %bitcast.13), channel_id=1, source_target_pairs={{0,1},{1,0},{2,3},{3,2},{4,5},{5,4},{6,7},{7,6},{8,9},{9,8},{10,11... | collective-permute-start | bytes 393224 | tf_op jit(solution)/shard_map/ppermute | solution.py:392
  39.4 16.7 %all-to-all-start.2 = ((f32[128,1,128]{2,1,0:T(1,128)}), f32[128,1,128]{2,1,0:T(1,128)S(1)}, u32[]{:S(2)}, u32[]{:S(2)}) async-start(f32[128,1,128]{2,1,0:T(1,128)} %bitcast.10), calls=%async_computation.2 | async-start | bytes 131072 | tf_op jit(solution)/shard_map/all_to_all | solution.py:396

commit v6 on v4

--- a/solution.py
+++ b/solution.py
@@ -22,6 +22,22 @@
 FOLDS = NFFT // FOLD
 
 
+FIRST = (2 * 8 + 5) * 4 + 2
+MEMBERS = list(range(CHANNELS))
+MEMBERS[0], MEMBERS[FIRST] = FIRST, 0
+
+
+def exchange(values):
+    return lax.all_to_all(values, "gx", 0, 0, axis_index_groups=[MEMBERS])
+
+
+def unswap(ref, rows):
+    here, there = slice(0, rows), slice(FIRST * rows, (FIRST + 1) * rows)
+    first, second = ref[here, :], ref[there, :]
+    ref[here, :] = second
+    ref[there, :] = first
+
+
 def split_bf16(values):
     high = values.astype(np.float32).astype(jnp.bfloat16)
     low = (values - high.astype(np.float64)).astype(np.float32).astype(jnp.bfloat16)
@@ -39,7 +55,7 @@
 
 
 def transform_weights():
-    odd = 2 * np.arange(CHANNELS) + 1
+    odd = 2 * np.array(MEMBERS) + 1
     phase = (odd[:, None] * np.arange(FOLD)[None, :]) % (2 * FOLD)
     angle = phase.astype(np.float64) * (2.0 * np.pi / (2 * FOLD))
     scale = 1.0 / math.sqrt(NFFT)
@@ -175,6 +191,7 @@
 
 def turn_spectra(source, wide_ref, real_ref, imag_ref):
     wide_ref[...] = source[...].astype(F32)
+    unswap(wide_ref, 4)
     for part, target in ((0, real_ref), (1, imag_ref)):
         for group in range(2):
             block = wide_ref[pl.ds(part * 2 + group, 128, 4), :].T
@@ -277,6 +294,7 @@
     wide_ref[0:8, :] = greal[0:OWNED, :]
     wide_ref[8:16, :] = gimag[0:OWNED, :]
     out_ref[...] = wide_ref[0:128, :].T
+    unswap(out_ref, 1)
 
 
 def solve(ownr, owni, other, model):
@@ -308,6 +326,7 @@
         for side, source in ((0, own_ref), (1, other_ref)):
             tile = half if side == 0 else 1 - half
             wide_ref[...] = source[...].astype(F32)
+            unswap(wide_ref, 4)
             for group in range(2):
                 real = wide_ref[pl.ds(group, 128, 4), :]
                 imag = wide_ref[pl.ds(2 + group, 128, 4), :]
@@ -355,26 +374,29 @@
     )(own, other)
 
 
-def turn_kernel(gains_ref, out_ref):
-    turned = gains_ref[...].T
+def turn_kernel(gains_ref, out_ref, rows_ref):
+    rows_ref[...] = gains_ref[...]
+    unswap(rows_ref, 1)
+    turned = rows_ref[...].T
     out_ref[0, 0] = turned[0:8, :]
     out_ref[1, 0] = turned[8:16, :]
 
 
 def on_device(voltages, model_magnitude, model_phase):
     spectra, model = channelize(voltages[0], model_magnitude, model_phase)
-    own = lax.all_to_all(spectra.reshape(CHANNELS, 4, 128), "gx", 0, 0)
+    own = exchange(spectra.reshape(CHANNELS, 4, 128))
     own, model = lax.optimization_barrier((own, model))
     own = own.reshape(512, 128)
     other = lax.ppermute(own, "bl", [(0, 1), (1, 0)])
     model = model.reshape(6, 128, OWNED).transpose(0, 2, 1).reshape(3 * TILES, 128)
     ownr, owni = own_turn(own)
     gains = solve(ownr, owni, other, model)
-    moved = lax.all_to_all(gains.reshape(128, 1, 128), "gx", 0, 0)
+    moved = exchange(gains.reshape(128, 1, 128))
     visible = power(own, other)
     gain_output = pl.pallas_call(
         turn_kernel,
         out_shape=jax.ShapeDtypeStruct((2, 1, OWNED, CHANNELS), F32),
+        scratch_shapes=[pltpu.VMEM((128, 128), F32)],
         compiler_params=pltpu.CompilerParams(vmem_limit_bytes=2 * 2**20),
         name="turn",
     )(moved.reshape(128, 128))

time: 52.6 us -> 50.3 us (0.956)
  starting transfers between devices: 8.21 us -> 15.6 us
  blocking collectives: 27.1 us -> 21 us
  waiting for transfers between devices: 4.12 us -> 0.49 us
    all_to_all x1, starting transfers between devices: 6.1 us -> 13.8 us  [exchange(): return lax.all_to_all(values, 'gx', 0, 0, axis_index_groups=[MEMBERS])]
    all_to_all x1, blocking collectives: 27.1 us -> 21 us  [exchange(): return lax.all_to_all(values, 'gx', 0, 0, axis_index_groups=[MEMBERS])]
    all_to_all x1, waiting for transfers between devices: 3.62 us -> 0.01 us  [exchange(): return lax.all_to_all(values, 'gx', 0, 0, axis_index_groups=[MEMBERS])]
  transfers between devices with their start and end apart: 2 -> 2, of which waited for: 2 -> 1; matrix products, arithmetic and copies ran while one was open for 1% -> 1% of each run, Pallas kernels for 13% -> 14%
where the time goes in v6:
time: 50.3 us; the launch traced here: 50.1 us
  blocking collectives  21 us (42%)
  starting transfers between devices  15.6 us (31%)
  Pallas kernels  12 us (24%)
  between operations  0.67 us (1%)
    all_to_all x1, blocking collectives, exchange(): return lax.all_to_all(values, 'gx', 0, 0, axis_index_groups=[MEMBERS])  21 us
    all_to_all x1, starting transfers between devices, exchange(): return lax.all_to_all(values, 'gx', 0, 0, axis_index_groups=[MEMBERS])  13.8 us
    pallas_call x1, Pallas kernels, power(): pl.pallas_call(power_kernel, grid=(1024 // ROWS,), in_specs=[pl.BlockSpec...  6.93 us
    pallas_call x1, Pallas kernels, channelize(): pl.pallas_call(channelize_kernel, out_shape=[pltpu.VMEM((CHANNELS * 4, 12...  2.41 us
    pallas_call x1, Pallas kernels, solve(): pl.pallas_call(solve_kernel, out_shape=pltpu.VMEM((128, 128), F32), scrat...  1.82 us
    ppermute x1, starting transfers between devices, on_device(): other = lax.ppermute(own, 'bl', [(0, 1), (1, 0)])  1.78 us
  transfers between devices with their start and end apart: 2, of which 1 were waited for; matrix products, arithmetic and copies ran while one was open for 1% of the time, Pallas kernels for 14%

profile of v6, /device:TPU:1, one launch (start us, length us, event | category | flops | bytes accessed | tf_op | source)
XLA Modules:
  0.0 50.1 jit_solution(1182846011196532465)
XLA Ops:
  0.6 2.4 %channelize.1 = (bf16[512,128]{1,0:T(8,128)(2,1)S(1)}, f32[48,128]{1,0:T(8,128)S(1)}) custom-call(bf16[8,71680]{1,0:T(8,128)(2,1)} %bitcast.20, f32[8,4,256]{2,1,0:T(4,128)} %constant.4.clone.window_hbm, bf16[256,512]{1,0:T(8,128)(2,1)} %constant.5.clone.table_hbm, f32[16,128]{1,0:T(8,128)} %bitcast.21, f32[16,128]{1,0:T(8,128)} %bitcast.22), custom_call_target="tpu_custom_call" | custom-call | tf_op jit(solution)/shard_map/channelize/pallas_call | solution.py:170
  3.0 21.0 %all_to_all.10 = bf16[128,4,128]{2,1,0:T(4,128)(2,1)S(1)} all-to-all(bf16[128,4,128]{2,1,0:T(4,128)(2,1)S(1)} %bitcast.16), channel_id=1, replica_groups={{172,2,4,6,8,10,12,14,16,18,20,22,24,26,28,30,32,34,36,38,40,42,44,46,4..., dimensions={0} | all-to-all | bytes 262144 | tf_op jit(solution)/shard_map/all_to_all | solution.py:31
  24.1 1.8 %collective-permute-start = (bf16[512,128]{1,0:T(8,128)(2,1)S(1)}, bf16[512,128]{1,0:T(8,128)(2,1)S(1)}, u32[]{:S(2)}, u32[]{:S(2)}) collective-permute-start(bf16[512,128]{1,0:T(8,128)(2,1)S(1)} %bitcast.12), channel_id=1, source_target_pairs={{0,1},{1,0},{2,3},{3,2},{4,5},{5,4},{6,7},{7,6},{8,9},{9,8},{10,11... | collective-permute-start | bytes 393224 | tf_op jit(solution)/shard_map/ppermute | solution.py:390
  25.9 0.2 reshape.32
  26.1 0.1 copy.9
  26.2 0.1 own_turn.1
  26.4 0.5 collective-permute-done.other_ref
  26.8 1.8 %solve.1 = f32[128,128]{1,0:T(8,128)} custom-call(f32[8,32,128]{2,1,0:T(8,128)S(1)} %get-tuple-element.11.ownr_ref, f32[8,32,128]{2,1,0:T(8,128)S(1)} %get-tuple-element.12.owni_ref, bf16[512,128]{1,0:T(8,128)(2,1)S(1)} %collective-permute-done.other_ref, f32[48,128]{1,0:T(8,128)S(1)} %bitcast.17), custom_call_target="tpu_custom_call" | custom-call | tf_op jit(solution)/shard_map/solve/pallas_call | solution.py:302
  28.7 13.8 %all-to-all-start.1 = ((f32[128,1,128]{2,1,0:T(1,128)}), f32[128,1,128]{2,1,0:T(1,128)S(1)}, u32[]{:S(2)}, u32[]{:S(2)}) async-start(f32[128,1,128]{2,1,0:T(1,128)} %bitcast.9), calls=%async_computation.1 | async-start | bytes 131072 | tf_op jit(solution)/shard_map/all_to_all | solution.py:31
  42.4 6.9 %power.1 = bf16[2,1024,2048]{2,1,0:T(8,128)(2,1)} custom-call(bf16[512,128]{1,0:T(8,128)(2,1)S(1)} %bitcast.14, bf16[512,128]{1,0:T(8,128)(2,1)S(1)} %collective-permute-done.other_ref), custom_call_target="tpu_custom_call" | custom-call | flops 536870912 | bytes 9437184 | tf_op jit(solution)/shard_map/power/pallas_call | solution.py:356
  49.4 0.0 all-to-all-done.1
  49.4 0.7 %turn.1 = f32[2,1,8,128]{3,2,1,0:T(8,128)} custom-call(f32[128,128]{1,0:T(8,128)S(1)} %bitcast.15), custom_call_target="tpu_custom_call" | custom-call | tf_op jit(solution)/shard_map/turn/pallas_call | solution.py:396
Async XLA Ops:
  24.1 2.8 %collective-permute-start = (bf16[512,128]{1,0:T(8,128)(2,1)S(1)}, bf16[512,128]{1,0:T(8,128)(2,1)S(1)}, u32[]{:S(2)}, u32[]{:S(2)}) collective-permute-start(bf16[512,128]{1,0:T(8,128)(2,1)S(1)} %bitcast.12), channel_id=1, source_target_pairs={{0,1},{1,0},{2,3},{3,2},{4,5},{5,4},{6,7},{7,6},{8,9},{9,8},{10,11... | collective-permute-start | bytes 393224 | tf_op jit(solution)/shard_map/ppermute | solution.py:390
  28.7 20.7 %all-to-all-start.1 = ((f32[128,1,128]{2,1,0:T(1,128)}), f32[128,1,128]{2,1,0:T(1,128)S(1)}, u32[]{:S(2)}, u32[]{:S(2)}) async-start(f32[128,1,128]{2,1,0:T(1,128)} %bitcast.9), calls=%async_computation.1 | async-start | bytes 131072 | tf_op jit(solution)/shard_map/all_to_all | solution.py:31

commit v7 on v6

--- a/solution.py
+++ b/solution.py
@@ -15,6 +15,7 @@
 ITERS = 4
 CHANNELS = 128
 OWNED = 8
+HALF = 1024
 EPSILON = 1e-06
 F32 = jnp.float32
 BF16 = jnp.bfloat16
@@ -199,16 +200,46 @@
                 target[group * 4 + j] = block[j * 32 : j * 32 + 32, :]
 
 
-def own_kernel(own_ref, real_ref, imag_ref, wide_ref):
+def build_lines(wide_ref, line_ref):
+    lane = lax.broadcasted_iota(jnp.int32, (128, 128), 1)
+    for group in range(2):
+        real = wide_ref[pl.ds(group, 128, 4), :]
+        imag = wide_ref[pl.ds(2 + group, 128, 4), :]
+        for j in range(4):
+            a = real if j == 0 else pltpu.roll(real, 128 - 32 * j, 1)
+            b = imag if j == 1 else pltpu.roll(imag, (160 - 32 * j) % 128, 1)
+            line_ref[pl.ds(group * 4 + j, 128, OWNED), :] = jnp.where(lane < 32, a, b)
+
+
+def build_right(line_ref, right_ref):
+    for block in range(HALF // 128):
+        columns = slice(block * 128, block * 128 + 128)
+        turned = line_ref[columns, :].T
+        real, imag = turned[0:32].astype(BF16), turned[32:64].astype(BF16)
+        right_ref[0, 0:32, columns] = real
+        right_ref[0, 32:64, columns] = imag
+        right_ref[1, 0:32, columns] = -imag
+        right_ref[1, 32:64, columns] = real
+
+
+def own_kernel(own_ref, real_ref, imag_ref, left_ref, right_ref, wide_ref, line_ref):
     turn_spectra(own_ref, wide_ref, real_ref, imag_ref)
+    build_lines(wide_ref, line_ref)
+    left_ref[...] = (line_ref[:, 0:64] * (1.0 / SPECTRA)).astype(BF16)
+    build_right(line_ref, right_ref)
 
 
 def own_turn(own):
     return pl.pallas_call(
         own_kernel,
-        out_shape=[jax.ShapeDtypeStruct((OWNED, SPECTRA, 128), F32)] * 2,
-        scratch_shapes=[pltpu.VMEM((512, 128), F32)],
-        compiler_params=pltpu.CompilerParams(vmem_limit_bytes=4 * 2**20),
+        out_shape=[
+            pltpu.VMEM((OWNED, SPECTRA, 128), F32),
+            pltpu.VMEM((OWNED, SPECTRA, 128), F32),
+            pltpu.VMEM((HALF, 2 * SPECTRA), BF16),
+            pltpu.VMEM((2, 2 * SPECTRA, HALF), BF16),
+        ],
+        scratch_shapes=[pltpu.VMEM((512, 128), F32), pltpu.VMEM((HALF, 128), F32)],
+        compiler_params=pltpu.CompilerParams(vmem_limit_bytes=8 * 2**20),
         cost_estimate=pl.CostEstimate(
             flops=2**22, bytes_accessed=2**20, transcendentals=0
         ),
@@ -314,64 +345,72 @@
     )(ownr, owni, other, model)
 
 
-ROWS = 128
-
-
-def power_kernel(own_ref, other_ref, out_ref, wide_ref, line_ref, upper_ref, lower_ref, right_ref):
+WIDE = 1024
+SLOTS = 4
+
+
+def power_kernel(
+    left_ref, mine_ref, other_ref, out_hbm, wide_ref, line_ref, right_ref, slots_ref, sems
+):
     half = lax.axis_index("bl")
-    step = pl.program_id(0)
-
-    @pl.when(step == 0)
-    def _():
-        for side, source in ((0, own_ref), (1, other_ref)):
-            tile = half if side == 0 else 1 - half
-            wide_ref[...] = source[...].astype(F32)
-            unswap(wide_ref, 4)
-            for group in range(2):
-                real = wide_ref[pl.ds(group, 128, 4), :]
-                imag = wide_ref[pl.ds(2 + group, 128, 4), :]
-                for j in range(4):
-                    a = real[:, j * 32 : j * 32 + 32]
-                    b = imag[:, j * 32 : j * 32 + 32]
-                    line_ref[pl.ds(group * 4 + j, 128, OWNED), :] = jnp.concatenate(
-                        [a, b, b, -a], axis=1
-                    )
-            lines = line_ref[...]
-            start = pl.multiple_of(tile * 1024, 1024)
-            right_ref[pl.ds(start, 1024), :] = lines[:, 0:64].astype(BF16)
-            if side == 0:
-                scaled = lines * (1.0 / SPECTRA)
-                upper_ref[...] = scaled[:, 0:64].astype(BF16)
-                lower_ref[...] = scaled[:, 64:128].astype(BF16)
-
-    rows = pl.ds(pl.multiple_of(step * ROWS, ROWS), ROWS)
-    for part, left in ((0, upper_ref), (1, lower_ref)):
-        out_ref[part] = lax.dot_general(
-            left[rows, :], right_ref[...], (((1,), (1,)), ((), ())),
-            preferred_element_type=F32,
-        ).astype(BF16)
-
-
-def power(own, other):
+    pieces = HALF // WIDE
+
+    def out_copy(count, part, start):
+        slot = lax.rem(count, SLOTS)
+        columns = pl.ds(pl.multiple_of(start, WIDE), WIDE)
+        return pltpu.make_async_copy(
+            slots_ref.at[slot], out_hbm.at[part, :, columns], sems.at[slot]
+        )
+
+    def products(right, side, done):
+        def step(index, carry):
+            part, piece = index // pieces, lax.rem(index, pieces)
+            count = done + index
+            first = pl.multiple_of(piece * WIDE, WIDE)
+            copy = out_copy(count, part, side * HALF + first)
+
+            @pl.when(count >= SLOTS)
+            def _():
+                copy.wait()
+
+            slots_ref[lax.rem(count, SLOTS)] = jnp.dot(
+                left_ref[...], right[part, :, pl.ds(first, WIDE)],
+                preferred_element_type=F32,
+            ).astype(BF16)
+            copy.start()
+            return carry
+
+        lax.fori_loop(0, 2 * pieces, step, 0)
+
+    products(mine_ref, half, 0)
+    wide_ref[...] = other_ref[...].astype(F32)
+    unswap(wide_ref, 4)
+    build_lines(wide_ref, line_ref)
+    build_right(line_ref, right_ref)
+    products(right_ref, 1 - half, 2 * pieces)
+    for slot in range(SLOTS):
+        out_copy(slot, 0, 0).wait()
+
+
+def power(left, mine, other):
     return pl.pallas_call(
         power_kernel,
-        grid=(1024 // ROWS,),
-        in_specs=[pl.BlockSpec((512, 128), lambda s: (0, 0))] * 2,
-        out_specs=pl.BlockSpec((2, ROWS, 2048), lambda s: (0, s, 0)),
-        out_shape=jax.ShapeDtypeStruct((2, 1024, 2048), BF16),
+        in_specs=[pl.BlockSpec(memory_space=pltpu.VMEM)] * 3,
+        out_specs=pl.BlockSpec(memory_space=pltpu.HBM),
+        out_shape=jax.ShapeDtypeStruct((2, HALF, 2 * HALF), BF16),
         scratch_shapes=[
             pltpu.VMEM((512, 128), F32),
-            pltpu.VMEM((1024, 128), F32),
-            pltpu.VMEM((1024, 64), BF16),
-            pltpu.VMEM((1024, 64), BF16),
-            pltpu.VMEM((2048, 64), BF16),
+            pltpu.VMEM((HALF, 128), F32),
+            pltpu.VMEM((2, 2 * SPECTRA, HALF), BF16),
+            pltpu.VMEM((SLOTS, HALF, WIDE), BF16),
+            pltpu.SemaphoreType.DMA((SLOTS,)),
         ],
         compiler_params=pltpu.CompilerParams(vmem_limit_bytes=24 * 2**20),
         cost_estimate=pl.CostEstimate(
             flops=2 * 2 * 1024 * 2048 * 64, bytes_accessed=9 * 2**20, transcendentals=0
         ),
         name="power",
-    )(own, other)
+    )(left, mine, other)
 
 
 def turn_kernel(gains_ref, out_ref, rows_ref):
@@ -389,10 +428,10 @@
     own = own.reshape(512, 128)
     other = lax.ppermute(own, "bl", [(0, 1), (1, 0)])
     model = model.reshape(6, 128, OWNED).transpose(0, 2, 1).reshape(3 * TILES, 128)
-    ownr, owni = own_turn(own)
+    ownr, owni, left, mine = own_turn(own)
     gains = solve(ownr, owni, other, model)
     moved = exchange(gains.reshape(128, 1, 128))
-    visible = power(own, other)
+    visible = power(left, mine, other)
     gain_output = pl.pallas_call(
         turn_kernel,
         out_shape=jax.ShapeDtypeStruct((2, 1, OWNED, CHANNELS), F32),

time: 50.3 us -> 47.8 us (0.950)
  Pallas kernels: 12 us -> 9.79 us
    pallas_call x2, Pallas kernels: 7.06 us -> 4.88 us  [the longest x1 4.46 us: power(): pl.pallas_call(power_kernel, in_specs=[pl.BlockSpec(memory_space=pltpu.VM...]
  transfers between devices with their start and end apart: 2 -> 2, of which waited for: 1 -> 1; matrix products, arithmetic and copies ran while one was open for 1% -> 1% of each run, Pallas kernels for 14% -> 10%
where the time goes in v7:
time: 47.8 us; the launch traced here: 47.6 us
  blocking collectives  21 us (44%)
  starting transfers between devices  15.6 us (33%)
  Pallas kernels  9.79 us (20%)
  between operations  0.68 us (1%)
    all_to_all x1, blocking collectives, exchange(): return lax.all_to_all(values, 'gx', 0, 0, axis_index_groups=[MEMBERS])  21 us
    all_to_all x1, starting transfers between devices, exchange(): return lax.all_to_all(values, 'gx', 0, 0, axis_index_groups=[MEMBERS])  13.8 us
    pallas_call x1, Pallas kernels, power(): pl.pallas_call(power_kernel, in_specs=[pl.BlockSpec(memory_space=pltpu.VM...  4.46 us
    pallas_call x1, Pallas kernels, channelize(): pl.pallas_call(channelize_kernel, out_shape=[pltpu.VMEM((CHANNELS * 4, 12...  2.41 us
    pallas_call x1, Pallas kernels, solve(): pl.pallas_call(solve_kernel, out_shape=pltpu.VMEM((128, 128), F32), scrat...  1.82 us
    ppermute x1, starting transfers between devices, on_device(): other = lax.ppermute(own, 'bl', [(0, 1), (1, 0)])  1.78 us
  transfers between devices with their start and end apart: 2, of which 1 were waited for; matrix products, arithmetic and copies ran while one was open for 1% of the time, Pallas kernels for 10%

profile of v7, /device:TPU:1, one launch (start us, length us, event | category | flops | bytes accessed | tf_op | source)
XLA Modules:
  0.0 47.6 jit_solution(13894499961049203108)
XLA Ops:
  0.6 2.4 %channelize.1 = (bf16[512,128]{1,0:T(8,128)(2,1)S(1)}, f32[48,128]{1,0:T(8,128)S(1)}) custom-call(bf16[8,71680]{1,0:T(8,128)(2,1)} %bitcast.19, f32[8,4,256]{2,1,0:T(4,128)} %constant.4.clone.window_hbm, bf16[256,512]{1,0:T(8,128)(2,1)} %constant.5.clone.table_hbm, f32[16,128]{1,0:T(8,128)} %bitcast.20, f32[16,128]{1,0:T(8,128)} %bitcast.21), custom_call_target="tpu_custom_call" | custom-call | tf_op jit(solution)/shard_map/channelize/pallas_call | solution.py:171
  3.0 21.0 %all_to_all.10 = bf16[128,4,128]{2,1,0:T(4,128)(2,1)S(1)} all-to-all(bf16[128,4,128]{2,1,0:T(4,128)(2,1)S(1)} %bitcast.15), channel_id=1, replica_groups={{172,2,4,6,8,10,12,14,16,18,20,22,24,26,28,30,32,34,36,38,40,42,44,46,4..., dimensions={0} | all-to-all | bytes 262144 | tf_op jit(solution)/shard_map/all_to_all | solution.py:32
  24.1 1.8 %collective-permute-start = (bf16[512,128]{1,0:T(8,128)(2,1)S(1)}, bf16[512,128]{1,0:T(8,128)(2,1)S(1)}, u32[]{:S(2)}, u32[]{:S(2)}) collective-permute-start(bf16[512,128]{1,0:T(8,128)(2,1)S(1)} %bitcast.12), channel_id=1, source_target_pairs={{0,1},{1,0},{2,3},{3,2},{4,5},{5,4},{6,7},{7,6},{8,9},{9,8},{10,11... | collective-permute-start | bytes 393224 | tf_op jit(solution)/shard_map/ppermute | solution.py:429
  25.9 0.2 reshape.32
  26.1 0.1 copy.9
  26.2 0.4 own_turn.1
  26.6 0.2 collective-permute-done.other_ref
  26.8 1.8 %solve.1 = f32[128,128]{1,0:T(8,128)} custom-call(f32[8,32,128]{2,1,0:T(8,128)S(1)} %get-tuple-element.15.ownr_ref, f32[8,32,128]{2,1,0:T(8,128)S(1)} %get-tuple-element.16.owni_ref, bf16[512,128]{1,0:T(8,128)(2,1)S(1)} %collective-permute-done.other_ref, f32[48,128]{1,0:T(8,128)S(1)} %bitcast.16), custom_call_target="tpu_custom_call" | custom-call | tf_op jit(solution)/shard_map/solve/pallas_call | solution.py:333
  28.7 13.8 %all-to-all-start.1 = ((f32[128,1,128]{2,1,0:T(1,128)}), f32[128,1,128]{2,1,0:T(1,128)S(1)}, u32[]{:S(2)}, u32[]{:S(2)}) async-start(f32[128,1,128]{2,1,0:T(1,128)} %bitcast.9), calls=%async_computation.1 | async-start | bytes 131072 | tf_op jit(solution)/shard_map/all_to_all | solution.py:32
  42.4 4.5 %power.1 = bf16[2,1024,2048]{2,1,0:T(8,128)(2,1)} custom-call(bf16[1024,64]{1,0:T(8,128)(2,1)S(1)} %get-tuple-element.13.left_ref, bf16[2,64,1024]{2,1,0:T(8,128)(2,1)S(1)} %get-tuple-element.14.mine_ref, bf16[512,128]{1,0:T(8,128)(2,1)S(1)} %collective-permute-done.other_ref), custom_call_target="tpu_custom_call" | custom-call | flops 536870912 | bytes 9437184 | tf_op jit(solution)/shard_map/power/pallas_call | solution.py:396
  46.9 0.0 all-to-all-done.1
  46.9 0.7 %turn.1 = f32[2,1,8,128]{3,2,1,0:T(8,128)} custom-call(f32[128,128]{1,0:T(8,128)S(1)} %bitcast.14), custom_call_target="tpu_custom_call" | custom-call | tf_op jit(solution)/shard_map/turn/pallas_call | solution.py:435
Async XLA Ops:
  24.1 2.8 %collective-permute-start = (bf16[512,128]{1,0:T(8,128)(2,1)S(1)}, bf16[512,128]{1,0:T(8,128)(2,1)S(1)}, u32[]{:S(2)}, u32[]{:S(2)}) collective-permute-start(bf16[512,128]{1,0:T(8,128)(2,1)S(1)} %bitcast.12), channel_id=1, source_target_pairs={{0,1},{1,0},{2,3},{3,2},{4,5},{5,4},{6,7},{7,6},{8,9},{9,8},{10,11... | collective-permute-start | bytes 393224 | tf_op jit(solution)/shard_map/ppermute | solution.py:429
  28.7 18.3 %all-to-all-start.1 = ((f32[128,1,128]{2,1,0:T(1,128)}), f32[128,1,128]{2,1,0:T(1,128)S(1)}, u32[]{:S(2)}, u32[]{:S(2)}) async-start(f32[128,1,128]{2,1,0:T(1,128)} %bitcast.9), calls=%async_computation.1 | async-start | bytes 131072 | tf_op jit(solution)/shard_map/all_to_all | solution.py:32

commit v8 on v7

--- a/solution.py
+++ b/solution.py
@@ -23,20 +23,25 @@
 FOLDS = NFFT // FOLD
 
 
-FIRST = (2 * 8 + 5) * 4 + 2
-MEMBERS = list(range(CHANNELS))
-MEMBERS[0], MEMBERS[FIRST] = FIRST, 0
-
-
-def exchange(values):
-    return lax.all_to_all(values, "gx", 0, 0, axis_index_groups=[MEMBERS])
-
-
-def unswap(ref, rows):
-    here, there = slice(0, rows), slice(FIRST * rows, (FIRST + 1) * rows)
-    first, second = ref[here, :], ref[there, :]
-    ref[here, :] = second
-    ref[there, :] = first
+SPECTRA_FIRST = 86
+GAINS_FIRST = 54
+
+
+def members(first):
+    order = list(range(CHANNELS))
+    order[0], order[first] = order[first], order[0]
+    return order
+
+
+def exchange(values, first):
+    return lax.all_to_all(values, "gx", 0, 0, axis_index_groups=[members(first)])
+
+
+def unswap(ref, rows, first):
+    here, there = slice(0, rows), slice(first * rows, (first + 1) * rows)
+    one, two = ref[here, :], ref[there, :]
+    ref[here, :] = two
+    ref[there, :] = one
 
 
 def split_bf16(values):
@@ -56,7 +61,7 @@
 
 
 def transform_weights():
-    odd = 2 * np.array(MEMBERS) + 1
+    odd = 2 * np.array(members(SPECTRA_FIRST)) + 1
     phase = (odd[:, None] * np.arange(FOLD)[None, :]) % (2 * FOLD)
     angle = phase.astype(np.float64) * (2.0 * np.pi / (2 * FOLD))
     scale = 1.0 / math.sqrt(NFFT)
@@ -72,7 +77,7 @@
 
 def channelize_kernel(
     volts_hbm, window_hbm, table_hbm, magnitude_hbm, phase_hbm, out_ref, model_ref,
-    volts_ref, window_ref, table_ref, magnitude_ref, phase_ref, folded_ref, rows_ref, sems,
+    volts_ref, window_ref, table_ref, folded_ref, rows_ref, sems,
 ):
     def frames_copy(first, count, slot):
         start = first * NFFT
@@ -89,21 +94,20 @@
         frames_copy(0, lead, GROUPS + 1),
     ]
     model_copies = [
-        pltpu.make_async_copy(magnitude_hbm, magnitude_ref, sems.at[GROUPS + 2]),
-        pltpu.make_async_copy(phase_hbm, phase_ref, sems.at[GROUPS + 3]),
+        pltpu.make_async_copy(
+            magnitude_hbm, model_ref.at[pl.ds(0, TILES), :], sems.at[GROUPS + 2]
+        ),
+        pltpu.make_async_copy(
+            phase_hbm, model_ref.at[pl.ds(TILES, TILES), :], sems.at[GROUPS + 3]
+        ),
     ]
     table_copy = pltpu.make_async_copy(table_hbm, table_ref, sems.at[GROUPS + 4])
-    for copy in model_copies + copies:
+    for copy in copies:
         copy.start()
     for group in range(GROUPS):
         frames_copy(group * GROUP + lead, GROUP, group).start()
-    table_copy.start()
-    for copy in model_copies:
-        copy.wait()
-    magnitude, phase = magnitude_ref[...], phase_ref[...]
-    model_ref[0:TILES, :] = magnitude * jnp.cos(phase)
-    model_ref[TILES : 2 * TILES, :] = magnitude * jnp.sin(phase)
-    model_ref[2 * TILES : 3 * TILES, :] = 1.0 / (magnitude * magnitude)
+    for copy in [table_copy] + model_copies:
+        copy.start()
     for copy in copies:
         copy.wait()
 
@@ -158,6 +162,8 @@
                 part * CHANNELS : (part + 1) * CHANNELS, side * 128 : side * 128 + 128
             ]
     out_ref[...] = rows_ref[...].astype(BF16)
+    for copy in model_copies:
+        copy.wait()
 
 
 def channelize(volts, magnitude, phase):
@@ -172,15 +178,13 @@
         channelize_kernel,
         out_shape=[
             pltpu.VMEM((CHANNELS * 4, 128), BF16),
-            pltpu.VMEM((3 * TILES, 128), F32),
+            pltpu.VMEM((2 * TILES, 128), F32),
         ],
         in_specs=[pl.BlockSpec(memory_space=pltpu.HBM)] * 5,
         scratch_shapes=[
             pltpu.VMEM(volts.shape, BF16),
             pltpu.VMEM((FOLDS, TAPS, FOLD), F32),
             pltpu.VMEM((2 * CHANNELS, 2 * FOLD), BF16),
-            pltpu.VMEM((TILES, 128), F32),
-            pltpu.VMEM((TILES, 128), F32),
             pltpu.VMEM((2, SPECTRA * OWNED, 128), F32),
             pltpu.VMEM((CHANNELS * 4, 128), F32),
             pltpu.SemaphoreType.DMA((GROUPS + 5,)),
@@ -192,7 +196,7 @@
 
 def turn_spectra(source, wide_ref, real_ref, imag_ref):
     wide_ref[...] = source[...].astype(F32)
-    unswap(wide_ref, 4)
+    unswap(wide_ref, 4, SPECTRA_FIRST)
     for part, target in ((0, real_ref), (1, imag_ref)):
         for group in range(2):
             block = wide_ref[pl.ds(part * 2 + group, 128, 4), :].T
@@ -222,14 +226,21 @@
         right_ref[1, 32:64, columns] = real
 
 
-def own_kernel(own_ref, real_ref, imag_ref, left_ref, right_ref, wide_ref, line_ref):
+def own_kernel(
+    own_ref, raw_ref, real_ref, imag_ref, left_ref, right_ref, model_ref,
+    wide_ref, line_ref,
+):
+    magnitude, phase = raw_ref[0:TILES, :], raw_ref[TILES : 2 * TILES, :]
+    model_ref[0:TILES, :] = magnitude * jnp.cos(phase)
+    model_ref[TILES : 2 * TILES, :] = magnitude * jnp.sin(phase)
+    model_ref[2 * TILES : 3 * TILES, :] = 1.0 / (magnitude * magnitude)
     turn_spectra(own_ref, wide_ref, real_ref, imag_ref)
     build_lines(wide_ref, line_ref)
     left_ref[...] = (line_ref[:, 0:64] * (1.0 / SPECTRA)).astype(BF16)
     build_right(line_ref, right_ref)
 
 
-def own_turn(own):
+def own_turn(own, raw):
     return pl.pallas_call(
         own_kernel,
         out_shape=[
@@ -237,6 +248,7 @@
             pltpu.VMEM((OWNED, SPECTRA, 128), F32),
             pltpu.VMEM((HALF, 2 * SPECTRA), BF16),
             pltpu.VMEM((2, 2 * SPECTRA, HALF), BF16),
+            pltpu.VMEM((3 * TILES, 128), F32),
         ],
         scratch_shapes=[pltpu.VMEM((512, 128), F32), pltpu.VMEM((HALF, 128), F32)],
         compiler_params=pltpu.CompilerParams(vmem_limit_bytes=8 * 2**20),
@@ -244,7 +256,7 @@
             flops=2**22, bytes_accessed=2**20, transcendentals=0
         ),
         name="own_turn",
-    )(own)
+    )(own, raw)
 
 
 def solve_kernel(
@@ -325,7 +337,7 @@
     wide_ref[0:8, :] = greal[0:OWNED, :]
     wide_ref[8:16, :] = gimag[0:OWNED, :]
     out_ref[...] = wide_ref[0:128, :].T
-    unswap(out_ref, 1)
+    unswap(out_ref, 1, GAINS_FIRST)
 
 
 def solve(ownr, owni, other, model):
@@ -384,7 +396,7 @@
 
     products(mine_ref, half, 0)
     wide_ref[...] = other_ref[...].astype(F32)
-    unswap(wide_ref, 4)
+    unswap(wide_ref, 4, SPECTRA_FIRST)
     build_lines(wide_ref, line_ref)
     build_right(line_ref, right_ref)
     products(right_ref, 1 - half, 2 * pieces)
@@ -415,22 +427,21 @@
 
 def turn_kernel(gains_ref, out_ref, rows_ref):
     rows_ref[...] = gains_ref[...]
-    unswap(rows_ref, 1)
+    unswap(rows_ref, 1, GAINS_FIRST)
     turned = rows_ref[...].T
     out_ref[0, 0] = turned[0:8, :]
     out_ref[1, 0] = turned[8:16, :]
 
 
 def on_device(voltages, model_magnitude, model_phase):
-    spectra, model = channelize(voltages[0], model_magnitude, model_phase)
-    own = exchange(spectra.reshape(CHANNELS, 4, 128))
-    own, model = lax.optimization_barrier((own, model))
+    spectra, raw = channelize(voltages[0], model_magnitude, model_phase)
+    own = exchange(spectra.reshape(CHANNELS, 4, 128), SPECTRA_FIRST)
     own = own.reshape(512, 128)
     other = lax.ppermute(own, "bl", [(0, 1), (1, 0)])
+    ownr, owni, left, mine, model = own_turn(own, raw)
     model = model.reshape(6, 128, OWNED).transpose(0, 2, 1).reshape(3 * TILES, 128)
-    ownr, owni, left, mine = own_turn(own)
     gains = solve(ownr, owni, other, model)
-    moved = exchange(gains.reshape(128, 1, 128))
+    moved = exchange(gains.reshape(128, 1, 128), GAINS_FIRST)
     visible = power(left, mine, other)
     gain_output = pl.pallas_call(
         turn_kernel,

time: 47.8 us -> 46.9 us (0.981)
  starting transfers between devices: 15.6 us -> 14.3 us
    all_to_all x1, starting transfers between devices: 13.8 us -> 12.6 us  [exchange(): lax.all_to_all(values, 'gx', 0, 0, axis_index_groups=[members(first)])]
  transfers between devices with their start and end apart: 2 -> 2, of which waited for: 1 -> 2; matrix products, arithmetic and copies ran while one was open for 1% -> 1% of each run, Pallas kernels for 10% -> 10%
where the time goes in v8:
time: 46.9 us; the launch traced here: 46.7 us
  blocking collectives  21 us (45%)
  starting transfers between devices  14.3 us (30%)
  Pallas kernels  9.74 us (21%)
  between operations  0.67 us (1%)
  waiting for transfers between devices  0.55 us (1%)
    all_to_all x1, blocking collectives, exchange(): lax.all_to_all(values, 'gx', 0, 0, axis_index_groups=[members(first)])  21 us
    all_to_all x1, starting transfers between devices, exchange(): lax.all_to_all(values, 'gx', 0, 0, axis_index_groups=[members(first)])  12.6 us
    pallas_call x1, Pallas kernels, power(): pl.pallas_call(power_kernel, in_specs=[pl.BlockSpec(memory_space=pltpu.VM...  4.46 us
    pallas_call x1, Pallas kernels, channelize(): pl.pallas_call(channelize_kernel, out_shape=[pltpu.VMEM((CHANNELS * 4, 12...  2.38 us
    pallas_call x1, Pallas kernels, solve(): pl.pallas_call(solve_kernel, out_shape=pltpu.VMEM((128, 128), F32), scrat...  1.82 us
    ppermute x1, starting transfers between devices, on_device(): other = lax.ppermute(own, 'bl', [(0, 1), (1, 0)])  1.78 us
  transfers between devices with their start and end apart: 2, of which 2 were waited for; matrix products, arithmetic and copies ran while one was open for 1% of the time, Pallas kernels for 10%

profile of v8, /device:TPU:1, one launch (start us, length us, event | category | flops | bytes accessed | tf_op | source)
XLA Modules:
  0.0 46.7 jit_solution(7521222102101073205)
XLA Ops:
  0.6 2.4 %channelize.1 = (bf16[512,128]{1,0:T(8,128)(2,1)S(1)}, f32[32,128]{1,0:T(8,128)S(1)}) custom-call(bf16[8,71680]{1,0:T(8,128)(2,1)} %bitcast.19, f32[8,4,256]{2,1,0:T(4,128)} %constant.4.clone.window_hbm, bf16[256,512]{1,0:T(8,128)(2,1)} %constant.5.clone.table_hbm, f32[16,128]{1,0:T(8,128)} %bitcast.20, f32[16,128]{1,0:T(8,128)} %bitcast.21), custom_call_target="tpu_custom_call" | custom-call | tf_op jit(solution)/shard_map/channelize/pallas_call | solution.py:177
  3.0 21.0 %all_to_all.10 = bf16[128,4,128]{2,1,0:T(4,128)(2,1)S(1)} all-to-all(bf16[128,4,128]{2,1,0:T(4,128)(2,1)S(1)} %bitcast.15), channel_id=1, replica_groups={{172,2,4,6,8,10,12,14,16,18,20,22,24,26,28,30,32,34,36,38,40,42,44,46,4..., dimensions={0} | all-to-all | bytes 262144 | tf_op jit(solution)/shard_map/all_to_all | solution.py:37
  24.0 1.8 %collective-permute-start = (bf16[512,128]{1,0:T(8,128)(2,1)S(1)}, bf16[512,128]{1,0:T(8,128)(2,1)S(1)}, u32[]{:S(2)}, u32[]{:S(2)}) collective-permute-start(bf16[512,128]{1,0:T(8,128)(2,1)S(1)} %bitcast.12), channel_id=1, source_target_pairs={{0,1},{1,0},{2,3},{3,2},{4,5},{5,4},{6,7},{7,6},{8,9},{9,8},{10,11... | collective-permute-start | bytes 393224 | tf_op jit(solution)/shard_map/ppermute | solution.py:440
  25.8 0.4 own_turn.1
  26.2 0.2 reshape.32
  26.5 0.1 copy.9
  26.6 0.2 collective-permute-done.other_ref
  26.8 1.8 %solve.1 = f32[128,128]{1,0:T(8,128)} custom-call(f32[8,32,128]{2,1,0:T(8,128)S(1)} %get-tuple-element.13.ownr_ref, f32[8,32,128]{2,1,0:T(8,128)S(1)} %get-tuple-element.14.owni_ref, bf16[512,128]{1,0:T(8,128)(2,1)S(1)} %collective-permute-done.other_ref, f32[48,128]{1,0:T(8,128)S(1)} %bitcast.16), custom_call_target="tpu_custom_call" | custom-call | tf_op jit(solution)/shard_map/solve/pallas_call | solution.py:345
  28.6 12.6 %all-to-all-start.1 = ((f32[128,1,128]{2,1,0:T(1,128)}), f32[128,1,128]{2,1,0:T(1,128)S(1)}, u32[]{:S(2)}, u32[]{:S(2)}) async-start(f32[128,1,128]{2,1,0:T(1,128)} %bitcast.9), calls=%async_computation.1 | async-start | bytes 131072 | tf_op jit(solution)/shard_map/all_to_all | solution.py:37
  41.2 4.5 %power.1 = bf16[2,1024,2048]{2,1,0:T(8,128)(2,1)} custom-call(bf16[1024,64]{1,0:T(8,128)(2,1)S(1)} %get-tuple-element.11.left_ref, bf16[2,64,1024]{2,1,0:T(8,128)(2,1)S(1)} %get-tuple-element.12.mine_ref, bf16[512,128]{1,0:T(8,128)(2,1)S(1)} %collective-permute-done.other_ref), custom_call_target="tpu_custom_call" | custom-call | flops 536870912 | bytes 9437184 | tf_op jit(solution)/shard_map/power/pallas_call | solution.py:408
  45.7 0.3 all-to-all-done.1
  46.0 0.7 %turn.1 = f32[2,1,8,128]{3,2,1,0:T(8,128)} custom-call(f32[128,128]{1,0:T(8,128)S(1)} %bitcast.14), custom_call_target="tpu_custom_call" | custom-call | tf_op jit(solution)/shard_map/turn/pallas_call | solution.py:446
Async XLA Ops:
  24.0 2.8 %collective-permute-start = (bf16[512,128]{1,0:T(8,128)(2,1)S(1)}, bf16[512,128]{1,0:T(8,128)(2,1)S(1)}, u32[]{:S(2)}, u32[]{:S(2)}) collective-permute-start(bf16[512,128]{1,0:T(8,128)(2,1)S(1)} %bitcast.12), channel_id=1, source_target_pairs={{0,1},{1,0},{2,3},{3,2},{4,5},{5,4},{6,7},{7,6},{8,9},{9,8},{10,11... | collective-permute-start | bytes 393224 | tf_op jit(solution)/shard_map/ppermute | solution.py:440
  28.6 17.4 %all-to-all-start.1 = ((f32[128,1,128]{2,1,0:T(1,128)}), f32[128,1,128]{2,1,0:T(1,128)S(1)}, u32[]{:S(2)}, u32[]{:S(2)}) async-start(f32[128,1,128]{2,1,0:T(1,128)} %bitcast.9), calls=%async_computation.1 | async-start | bytes 131072 | tf_op jit(solution)/shard_map/all_to_all | solution.py:37

commit v9 on v8

--- a/solution.py
+++ b/solution.py
@@ -23,7 +23,7 @@
 FOLDS = NFFT // FOLD
 
 
-SPECTRA_FIRST = 86
+SPECTRA_FIRST = 90
 GAINS_FIRST = 54
 
 
@@ -80,10 +80,7 @@
     volts_ref, window_ref, table_ref, folded_ref, rows_ref, sems,
 ):
     def frames_copy(first, count, slot):
-        start = first * NFFT
-        if not isinstance(first, int):
-            start = pl.multiple_of(start, NFFT)
-        span = pl.ds(start, count * NFFT)
+        span = pl.ds(first * NFFT, count * NFFT)
         return pltpu.make_async_copy(
             volts_hbm.at[:, span], volts_ref.at[:, span], sems.at[slot]
         )
@@ -111,7 +108,7 @@
     for copy in copies:
         copy.wait()
 
-    def group_step(group, carry):
+    def group_step(group):
         first = group * GROUP
         frames_copy(first + lead, GROUP, group).wait()
         for part in range(FOLD // 128):
@@ -124,18 +121,18 @@
                 ]
                 for frame in range(GROUP + TAPS - 1):
                     offset = (first + frame) * NFFT + fold * FOLD + part * 128
-                    piece = volts_ref[:, pl.ds(pl.multiple_of(offset, 128), 128)]
+                    piece = volts_ref[:, pl.ds(offset, 128)]
                     piece = piece.astype(F32)
                     for tap in range(TAPS):
                         s = frame - tap
                         if 0 <= s < GROUP:
                             sums[s] = sums[s] + piece * taps[tap]
             for s in range(GROUP):
-                row = pl.multiple_of((first + s) * OWNED, OWNED)
+                row = (first + s) * OWNED
                 folded_ref[part, pl.ds(row, OWNED), :] = sums[s]
-        return carry
-
-    lax.fori_loop(0, GROUPS, group_step, 0)
+
+    for group in range(GROUPS):
+        group_step(group)
     pieces = []
     for part in range(FOLD // 128):
         pieces.append(

time: 46.9 us -> 46.7 us (level)
  no operation moved by 1% of the time
where the time goes in v9:
time: 46.7 us; the launch traced here: 46.4 us
  blocking collectives  21.2 us (45%)
  starting transfers between devices  14.1 us (30%)
  Pallas kernels  9.53 us (20%)
  between operations  0.67 us (1%)
  waiting for transfers between devices  0.55 us (1%)
    all_to_all x1, blocking collectives, exchange(): lax.all_to_all(values, 'gx', 0, 0, axis_index_groups=[members(first)])  21.2 us
    all_to_all x1, starting transfers between devices, exchange(): lax.all_to_all(values, 'gx', 0, 0, axis_index_groups=[members(first)])  12.3 us
    pallas_call x1, Pallas kernels, power(): pl.pallas_call(power_kernel, in_specs=[pl.BlockSpec(memory_space=pltpu.VM...  4.46 us
    pallas_call x1, Pallas kernels, channelize(): pl.pallas_call(channelize_kernel, out_shape=[pltpu.VMEM((CHANNELS * 4, 12...  2.17 us
    ppermute x1, starting transfers between devices, on_device(): other = lax.ppermute(own, 'bl', [(0, 1), (1, 0)])  1.82 us
    pallas_call x1, Pallas kernels, solve(): pl.pallas_call(solve_kernel, out_shape=pltpu.VMEM((128, 128), F32), scrat...  1.82 us
  transfers between devices with their start and end apart: 2, of which 2 were waited for; matrix products, arithmetic and copies ran while one was open for 1% of the time, Pallas kernels for 10%

profile of v9, /device:TPU:1, one launch (start us, length us, event | category | flops | bytes accessed | tf_op | source)
XLA Modules:
  0.0 46.4 jit_solution(16399169454461350991)
XLA Ops:
  0.6 2.2 %channelize.1 = (bf16[512,128]{1,0:T(8,128)(2,1)S(1)}, f32[32,128]{1,0:T(8,128)S(1)}) custom-call(bf16[8,71680]{1,0:T(8,128)(2,1)} %bitcast.19, f32[8,4,256]{2,1,0:T(4,128)} %constant.4.clone.window_hbm, bf16[256,512]{1,0:T(8,128)(2,1)} %constant.5.clone.table_hbm, f32[16,128]{1,0:T(8,128)} %bitcast.20, f32[16,128]{1,0:T(8,128)} %bitcast.21), custom_call_target="tpu_custom_call" | custom-call | tf_op jit(solution)/shard_map/channelize/pallas_call | solution.py:174
  2.8 21.2 %all_to_all.10 = bf16[128,4,128]{2,1,0:T(4,128)(2,1)S(1)} all-to-all(bf16[128,4,128]{2,1,0:T(4,128)(2,1)S(1)} %bitcast.15), channel_id=1, replica_groups={{180,2,4,6,8,10,12,14,16,18,20,22,24,26,28,30,32,34,36,38,40,42,44,46,4..., dimensions={0} | all-to-all | bytes 262144 | tf_op jit(solution)/shard_map/all_to_all | solution.py:37
  24.1 1.8 %collective-permute-start = (bf16[512,128]{1,0:T(8,128)(2,1)S(1)}, bf16[512,128]{1,0:T(8,128)(2,1)S(1)}, u32[]{:S(2)}, u32[]{:S(2)}) collective-permute-start(bf16[512,128]{1,0:T(8,128)(2,1)S(1)} %bitcast.12), channel_id=1, source_target_pairs={{0,1},{1,0},{2,3},{3,2},{4,5},{5,4},{6,7},{7,6},{8,9},{9,8},{10,11... | collective-permute-start | bytes 393224 | tf_op jit(solution)/shard_map/ppermute | solution.py:437
  25.9 0.4 own_turn.1
  26.3 0.2 reshape.32
  26.5 0.1 copy.9
  26.6 0.2 collective-permute-done.other_ref
  26.9 1.8 %solve.1 = f32[128,128]{1,0:T(8,128)} custom-call(f32[8,32,128]{2,1,0:T(8,128)S(1)} %get-tuple-element.13.ownr_ref, f32[8,32,128]{2,1,0:T(8,128)S(1)} %get-tuple-element.14.owni_ref, bf16[512,128]{1,0:T(8,128)(2,1)S(1)} %collective-permute-done.other_ref, f32[48,128]{1,0:T(8,128)S(1)} %bitcast.16), custom_call_target="tpu_custom_call" | custom-call | tf_op jit(solution)/shard_map/solve/pallas_call | solution.py:342
  28.7 12.3 %all-to-all-start.1 = ((f32[128,1,128]{2,1,0:T(1,128)}), f32[128,1,128]{2,1,0:T(1,128)S(1)}, u32[]{:S(2)}, u32[]{:S(2)}) async-start(f32[128,1,128]{2,1,0:T(1,128)} %bitcast.9), calls=%async_computation.1 | async-start | bytes 131072 | tf_op jit(solution)/shard_map/all_to_all | solution.py:37
  40.9 4.5 %power.1 = bf16[2,1024,2048]{2,1,0:T(8,128)(2,1)} custom-call(bf16[1024,64]{1,0:T(8,128)(2,1)S(1)} %get-tuple-element.11.left_ref, bf16[2,64,1024]{2,1,0:T(8,128)(2,1)S(1)} %get-tuple-element.12.mine_ref, bf16[512,128]{1,0:T(8,128)(2,1)S(1)} %collective-permute-done.other_ref), custom_call_target="tpu_custom_call" | custom-call | flops 536870912 | bytes 9437184 | tf_op jit(solution)/shard_map/power/pallas_call | solution.py:405
  45.4 0.3 all-to-all-done.1
  45.7 0.7 %turn.1 = f32[2,1,8,128]{3,2,1,0:T(8,128)} custom-call(f32[128,128]{1,0:T(8,128)S(1)} %bitcast.14), custom_call_target="tpu_custom_call" | custom-call | tf_op jit(solution)/shard_map/turn/pallas_call | solution.py:443
Async XLA Ops:
  24.1 2.8 %collective-permute-start = (bf16[512,128]{1,0:T(8,128)(2,1)S(1)}, bf16[512,128]{1,0:T(8,128)(2,1)S(1)}, u32[]{:S(2)}, u32[]{:S(2)}) collective-permute-start(bf16[512,128]{1,0:T(8,128)(2,1)S(1)} %bitcast.12), channel_id=1, source_target_pairs={{0,1},{1,0},{2,3},{3,2},{4,5},{5,4},{6,7},{7,6},{8,9},{9,8},{10,11... | collective-permute-start | bytes 393224 | tf_op jit(solution)/shard_map/ppermute | solution.py:437
  28.7 17.1 %all-to-all-start.1 = ((f32[128,1,128]{2,1,0:T(1,128)}), f32[128,1,128]{2,1,0:T(1,128)S(1)}, u32[]{:S(2)}, u32[]{:S(2)}) async-start(f32[128,1,128]{2,1,0:T(1,128)} %bitcast.9), calls=%async_computation.1 | async-start | bytes 131072 | tf_op jit(solution)/shard_map/all_to_all | solution.py:37

commit v10 on v9

--- a/solution.py
+++ b/solution.py
@@ -324,12 +324,10 @@
     greal = jnp.ones((tiles, 128), F32)
     gimag = jnp.zeros((tiles, 128), F32)
 
-    def double_step(_, gains):
-        first = single_step(*gains)
+    for _ in range(ITERS // 2):
+        first = single_step(greal, gimag)
         fresh = single_step(*first)
-        return tuple((a + b) * 0.5 for a, b in zip(fresh, first))
-
-    greal, gimag = lax.fori_loop(0, ITERS // 2, double_step, (greal, gimag))
+        greal, gimag = [(a + b) * 0.5 for a, b in zip(fresh, first)]
     wide_ref[0:128, :] = jnp.zeros((128, 128), F32)
     wide_ref[0:8, :] = greal[0:OWNED, :]
     wide_ref[8:16, :] = gimag[0:OWNED, :]

time: 46.7 us -> 46.5 us (level)
  transfers between devices with their start and end apart: 2 -> 2, of which waited for: 2 -> 2; matrix products, arithmetic and copies ran while one was open for 1% -> 1% of each run, Pallas kernels for 10% -> 11%
where the time goes in v10:
time: 46.5 us; the launch traced here: 46.3 us
  blocking collectives  21.2 us (46%)
  starting transfers between devices  14.1 us (30%)
  Pallas kernels  9.41 us (20%)
  between operations  0.67 us (1%)
  waiting for transfers between devices  0.55 us (1%)
    all_to_all x1, blocking collectives, exchange(): lax.all_to_all(values, 'gx', 0, 0, axis_index_groups=[members(first)])  21.2 us
    all_to_all x1, starting transfers between devices, exchange(): lax.all_to_all(values, 'gx', 0, 0, axis_index_groups=[members(first)])  12.3 us
    pallas_call x1, Pallas kernels, power(): pl.pallas_call(power_kernel, in_specs=[pl.BlockSpec(memory_space=pltpu.VM...  4.46 us
    pallas_call x1, Pallas kernels, channelize(): pl.pallas_call(channelize_kernel, out_shape=[pltpu.VMEM((CHANNELS * 4, 12...  2.17 us
    ppermute x1, starting transfers between devices, on_device(): other = lax.ppermute(own, 'bl', [(0, 1), (1, 0)])  1.82 us
    pallas_call x1, Pallas kernels, solve(): pl.pallas_call(solve_kernel, out_shape=pltpu.VMEM((128, 128), F32), scrat...  1.7 us
  transfers between devices with their start and end apart: 2, of which 2 were waited for; matrix products, arithmetic and copies ran while one was open for 1% of the time, Pallas kernels for 11%

profile of v10, /device:TPU:1, one launch (start us, length us, event | category | flops | bytes accessed | tf_op | source)
XLA Modules:
  0.0 46.3 jit_solution(14376476413352160052)
XLA Ops:
  0.6 2.2 %channelize.1 = (bf16[512,128]{1,0:T(8,128)(2,1)S(1)}, f32[32,128]{1,0:T(8,128)S(1)}) custom-call(bf16[8,71680]{1,0:T(8,128)(2,1)} %bitcast.19, f32[8,4,256]{2,1,0:T(4,128)} %constant.4.clone.window_hbm, bf16[256,512]{1,0:T(8,128)(2,1)} %constant.5.clone.table_hbm, f32[16,128]{1,0:T(8,128)} %bitcast.20, f32[16,128]{1,0:T(8,128)} %bitcast.21), custom_call_target="tpu_custom_call" | custom-call | tf_op jit(solution)/shard_map/channelize/pallas_call | solution.py:174
  2.8 21.2 %all_to_all.10 = bf16[128,4,128]{2,1,0:T(4,128)(2,1)S(1)} all-to-all(bf16[128,4,128]{2,1,0:T(4,128)(2,1)S(1)} %bitcast.15), channel_id=1, replica_groups={{180,2,4,6,8,10,12,14,16,18,20,22,24,26,28,30,32,34,36,38,40,42,44,46,4..., dimensions={0} | all-to-all | bytes 262144 | tf_op jit(solution)/shard_map/all_to_all | solution.py:37
  24.1 1.8 %collective-permute-start = (bf16[512,128]{1,0:T(8,128)(2,1)S(1)}, bf16[512,128]{1,0:T(8,128)(2,1)S(1)}, u32[]{:S(2)}, u32[]{:S(2)}) collective-permute-start(bf16[512,128]{1,0:T(8,128)(2,1)S(1)} %bitcast.12), channel_id=1, source_target_pairs={{0,1},{1,0},{2,3},{3,2},{4,5},{5,4},{6,7},{7,6},{8,9},{9,8},{10,11... | collective-permute-start | bytes 393224 | tf_op jit(solution)/shard_map/ppermute | solution.py:435
  25.9 0.4 own_turn.1
  26.3 0.2 reshape.32
  26.5 0.1 copy.9
  26.6 0.2 collective-permute-done.other_ref
  26.9 1.7 %solve.1 = f32[128,128]{1,0:T(8,128)} custom-call(f32[8,32,128]{2,1,0:T(8,128)S(1)} %get-tuple-element.13.ownr_ref, f32[8,32,128]{2,1,0:T(8,128)S(1)} %get-tuple-element.14.owni_ref, bf16[512,128]{1,0:T(8,128)(2,1)S(1)} %collective-permute-done.other_ref, f32[48,128]{1,0:T(8,128)S(1)} %bitcast.16), custom_call_target="tpu_custom_call" | custom-call | tf_op jit(solution)/shard_map/solve/pallas_call | solution.py:340
  28.6 12.3 %all-to-all-start.1 = ((f32[128,1,128]{2,1,0:T(1,128)}), f32[128,1,128]{2,1,0:T(1,128)S(1)}, u32[]{:S(2)}, u32[]{:S(2)}) async-start(f32[128,1,128]{2,1,0:T(1,128)} %bitcast.9), calls=%async_computation.1 | async-start | bytes 131072 | tf_op jit(solution)/shard_map/all_to_all | solution.py:37
  40.8 4.5 %power.1 = bf16[2,1024,2048]{2,1,0:T(8,128)(2,1)} custom-call(bf16[1024,64]{1,0:T(8,128)(2,1)S(1)} %get-tuple-element.11.left_ref, bf16[2,64,1024]{2,1,0:T(8,128)(2,1)S(1)} %get-tuple-element.12.mine_ref, bf16[512,128]{1,0:T(8,128)(2,1)S(1)} %collective-permute-done.other_ref), custom_call_target="tpu_custom_call" | custom-call | flops 536870912 | bytes 9437184 | tf_op jit(solution)/shard_map/power/pallas_call | solution.py:403
  45.3 0.3 all-to-all-done.1
  45.6 0.7 %turn.1 = f32[2,1,8,128]{3,2,1,0:T(8,128)} custom-call(f32[128,128]{1,0:T(8,128)S(1)} %bitcast.14), custom_call_target="tpu_custom_call" | custom-call | tf_op jit(solution)/shard_map/turn/pallas_call | solution.py:441
Async XLA Ops:
  24.1 2.8 %collective-permute-start = (bf16[512,128]{1,0:T(8,128)(2,1)S(1)}, bf16[512,128]{1,0:T(8,128)(2,1)S(1)}, u32[]{:S(2)}, u32[]{:S(2)}) collective-permute-start(bf16[512,128]{1,0:T(8,128)(2,1)S(1)} %bitcast.12), channel_id=1, source_target_pairs={{0,1},{1,0},{2,3},{3,2},{4,5},{5,4},{6,7},{7,6},{8,9},{9,8},{10,11... | collective-permute-start | bytes 393224 | tf_op jit(solution)/shard_map/ppermute | solution.py:435
  28.6 17.1 %all-to-all-start.1 = ((f32[128,1,128]{2,1,0:T(1,128)}), f32[128,1,128]{2,1,0:T(1,128)S(1)}, u32[]{:S(2)}, u32[]{:S(2)}) async-start(f32[128,1,128]{2,1,0:T(1,128)} %bitcast.9), calls=%async_computation.1 | async-start | bytes 131072 | tf_op jit(solution)/shard_map/all_to_all | solution.py:37

commit v11 on v10

--- a/solution.py
+++ b/solution.py
@@ -24,7 +24,7 @@
 
 
 SPECTRA_FIRST = 90
-GAINS_FIRST = 54
+GAINS_FIRST = 22
 
 
 def members(first):

time: 46.5 us -> 46.5 us (level)
  transfers between devices with their start and end apart: 2 -> 2, of which waited for: 2 -> 2; matrix products, arithmetic and copies ran while one was open for 1% -> 1% of each run, Pallas kernels for 11% -> 10%
where the time goes in v11:
time: 46.5 us; the launch traced here: 46.3 us
  blocking collectives  21.2 us (46%)
  starting transfers between devices  13.8 us (30%)
  Pallas kernels  9.4 us (20%)
  waiting for transfers between devices  0.85 us (2%)
  between operations  0.67 us (1%)
    all_to_all x1, blocking collectives, exchange(): lax.all_to_all(values, 'gx', 0, 0, axis_index_groups=[members(first)])  21.2 us
    all_to_all x1, starting transfers between devices, exchange(): lax.all_to_all(values, 'gx', 0, 0, axis_index_groups=[members(first)])  11.9 us
    pallas_call x1, Pallas kernels, power(): pl.pallas_call(power_kernel, in_specs=[pl.BlockSpec(memory_space=pltpu.VM...  4.45 us
    pallas_call x1, Pallas kernels, channelize(): pl.pallas_call(channelize_kernel, out_shape=[pltpu.VMEM((CHANNELS * 4, 12...  2.17 us
    ppermute x1, starting transfers between devices, on_device(): other = lax.ppermute(own, 'bl', [(0, 1), (1, 0)])  1.82 us
    pallas_call x1, Pallas kernels, solve(): pl.pallas_call(solve_kernel, out_shape=pltpu.VMEM((128, 128), F32), scrat...  1.7 us
  transfers between devices with their start and end apart: 2, of which 2 were waited for; matrix products, arithmetic and copies ran while one was open for 1% of the time, Pallas kernels for 10%

profile of v11, /device:TPU:1, one launch (start us, length us, event | category | flops | bytes accessed | tf_op | source)
XLA Modules:
  0.0 46.3 jit_solution(17881165103218387303)
XLA Ops:
  0.6 2.2 %channelize.1 = (bf16[512,128]{1,0:T(8,128)(2,1)S(1)}, f32[32,128]{1,0:T(8,128)S(1)}) custom-call(bf16[8,71680]{1,0:T(8,128)(2,1)} %bitcast.19, f32[8,4,256]{2,1,0:T(4,128)} %constant.4.clone.window_hbm, bf16[256,512]{1,0:T(8,128)(2,1)} %constant.5.clone.table_hbm, f32[16,128]{1,0:T(8,128)} %bitcast.20, f32[16,128]{1,0:T(8,128)} %bitcast.21), custom_call_target="tpu_custom_call" | custom-call | tf_op jit(solution)/shard_map/channelize/pallas_call | solution.py:174
  2.8 21.2 %all_to_all.10 = bf16[128,4,128]{2,1,0:T(4,128)(2,1)S(1)} all-to-all(bf16[128,4,128]{2,1,0:T(4,128)(2,1)S(1)} %bitcast.15), channel_id=1, replica_groups={{180,2,4,6,8,10,12,14,16,18,20,22,24,26,28,30,32,34,36,38,40,42,44,46,4..., dimensions={0} | all-to-all | bytes 262144 | tf_op jit(solution)/shard_map/all_to_all | solution.py:37
  24.1 1.8 %collective-permute-start = (bf16[512,128]{1,0:T(8,128)(2,1)S(1)}, bf16[512,128]{1,0:T(8,128)(2,1)S(1)}, u32[]{:S(2)}, u32[]{:S(2)}) collective-permute-start(bf16[512,128]{1,0:T(8,128)(2,1)S(1)} %bitcast.12), channel_id=1, source_target_pairs={{0,1},{1,0},{2,3},{3,2},{4,5},{5,4},{6,7},{7,6},{8,9},{9,8},{10,11... | collective-permute-start | bytes 393224 | tf_op jit(solution)/shard_map/ppermute | solution.py:435
  25.9 0.4 own_turn.1
  26.3 0.2 reshape.32
  26.5 0.1 copy.9
  26.6 0.2 collective-permute-done.other_ref
  26.9 1.7 %solve.1 = f32[128,128]{1,0:T(8,128)} custom-call(f32[8,32,128]{2,1,0:T(8,128)S(1)} %get-tuple-element.13.ownr_ref, f32[8,32,128]{2,1,0:T(8,128)S(1)} %get-tuple-element.14.owni_ref, bf16[512,128]{1,0:T(8,128)(2,1)S(1)} %collective-permute-done.other_ref, f32[48,128]{1,0:T(8,128)S(1)} %bitcast.16), custom_call_target="tpu_custom_call" | custom-call | tf_op jit(solution)/shard_map/solve/pallas_call | solution.py:340
  28.6 11.9 %all-to-all-start.1 = ((f32[128,1,128]{2,1,0:T(1,128)}), f32[128,1,128]{2,1,0:T(1,128)S(1)}, u32[]{:S(2)}, u32[]{:S(2)}) async-start(f32[128,1,128]{2,1,0:T(1,128)} %bitcast.9), calls=%async_computation.1 | async-start | bytes 131072 | tf_op jit(solution)/shard_map/all_to_all | solution.py:37
  40.5 4.5 %power.1 = bf16[2,1024,2048]{2,1,0:T(8,128)(2,1)} custom-call(bf16[1024,64]{1,0:T(8,128)(2,1)S(1)} %get-tuple-element.11.left_ref, bf16[2,64,1024]{2,1,0:T(8,128)(2,1)S(1)} %get-tuple-element.12.mine_ref, bf16[512,128]{1,0:T(8,128)(2,1)S(1)} %collective-permute-done.other_ref), custom_call_target="tpu_custom_call" | custom-call | flops 536870912 | bytes 9437184 | tf_op jit(solution)/shard_map/power/pallas_call | solution.py:403
  45.0 0.6 %all-to-all-done.1 = f32[128,1,128]{2,1,0:T(1,128)S(1)} async-done(((f32[128,1,128]{2,1,0:T(1,128)}), f32[128,1,128]{2,1,0:T(1,128)S(1)}, u32[]{:S(2)}, u32[]{:S(2)}) %all-to-all-start.1) | async-done | bytes 65568 | tf_op jit(solution)/shard_map/all_to_all | solution.py:37
  45.6 0.7 %turn.1 = f32[2,1,8,128]{3,2,1,0:T(8,128)} custom-call(f32[128,128]{1,0:T(8,128)S(1)} %bitcast.14), custom_call_target="tpu_custom_call" | custom-call | tf_op jit(solution)/shard_map/turn/pallas_call | solution.py:441
Async XLA Ops:
  24.1 2.8 %collective-permute-start = (bf16[512,128]{1,0:T(8,128)(2,1)S(1)}, bf16[512,128]{1,0:T(8,128)(2,1)S(1)}, u32[]{:S(2)}, u32[]{:S(2)}) collective-permute-start(bf16[512,128]{1,0:T(8,128)(2,1)S(1)} %bitcast.12), channel_id=1, source_target_pairs={{0,1},{1,0},{2,3},{3,2},{4,5},{5,4},{6,7},{7,6},{8,9},{9,8},{10,11... | collective-permute-start | bytes 393224 | tf_op jit(solution)/shard_map/ppermute | solution.py:435
  28.6 17.0 %all-to-all-start.1 = ((f32[128,1,128]{2,1,0:T(1,128)}), f32[128,1,128]{2,1,0:T(1,128)S(1)}, u32[]{:S(2)}, u32[]{:S(2)}) async-start(f32[128,1,128]{2,1,0:T(1,128)} %bitcast.9), calls=%async_computation.1 | async-start | bytes 131072 | tf_op jit(solution)/shard_map/all_to_all | solution.py:37
